TPU v7x, 512 devices: a whole 4x8x8 slice. The times are simulated.
512 devices in a mesh: grp: 128 (over y, x, z_hi, core), qtr: 4 (over z_lo).
Axes of the slice: x: 4, y: 8, z: 8 (z_hi: 2, z_lo: 4; z = z_hi * 4 + z_lo), core: 2. Of those that a mesh axis runs over, the one named last changes fastest.
Arguments:
- vectors: float32 [131072, 512], P(('grp', 'qtr')), may hold values from -6 to 6
- previous: float32 [131072, 512], P(('grp', 'qtr')), may hold values from -6 to 6
- diag_tiles: bfloat16 [1024, 4, 128, 128], P(('grp', 'qtr')), may hold values from -0.125 to 0.125
- diag_cols: int32 [1024, 4], P(('grp', 'qtr')), may hold values from 0 to 7, all different within a row
- diag_mask: int32 [1024, 4], P(('grp', 'qtr')), may hold values 0 or 1
- off_tiles: bfloat16 [3, 1024, 4, 128, 128], P(None, ('grp', 'qtr')), may hold values from -0.125 to 0.125
- off_rows: int32 [3, 1024, 4], P(None, ('grp', 'qtr')), may hold values from 0 to 7, all different within a row
- off_mask: int32 [3, 1024, 4], P(None, ('grp', 'qtr')), may hold values 0 or 1
Outputs:
- chebyshev: float32 [131072, 512], P(('grp', 'qtr'))
Inputs may be any that keep to these rules, and one draw needn't show every extreme that they name: `diag_cols`: each row names 4 different tile columns of the group. `off_rows`: each row names 4 different tile rows of the group.
All inputs are finite; a program needn't handle non-finite values. No bound on the sum of `diag_mask` or of `off_mask` on one device may be relied on, other than what follows from the above.
Results may differ from a plain program's by a relative error of at most 0.002.
Values may be sent and summed in bfloat16 or wider, within the bound.
No kernel may reach another device: no remote copies, remote signals or barrier semaphores. Data moves between devices by JAX's collectives and lax.ppermute only.
A program may use at most 64 MiB of HBM per device.

v0:
```python
import jax
import jax.numpy as jnp
from jax import lax
from jax.experimental import pallas as pl
from jax.experimental.pallas import tpu as pltpu
from jax.sharding import PartitionSpec as P


cheb_center = 0.25
cheb_half = 2.0


def swap(block, axis, mask):
    count = lax.axis_size(axis)
    return lax.ppermute(block, axis, [(i, i ^ mask) for i in range(count)])


def live(tile, flag):
    return (tile.astype(jnp.float32) * flag.astype(jnp.float32)).astype(jnp.bfloat16)


def dot_plain(a, b):
    return lax.dot_general(a, b, (((1,), (0,)), ((), ())), preferred_element_type=jnp.float32)


def dot_flipped(a, b):
    return lax.dot_general(a, b, (((0,), (0,)), ((), ())), preferred_element_type=jnp.float32)


def spread_add(acc, tiles, flags, places, flipped, block, shift):
    slots, size, _ = tiles.shape
    for slot in range(slots):
        place = pl.multiple_of((places(slot) ^ shift) * size, size)
        tile = live(tiles[slot], flags(slot))
        product = dot_flipped(tile, block) if flipped else dot_plain(tile, block)
        acc[pl.ds(place, size), :] += product


def scatter_kernel(
    diag_cols, diag_mask, off_rows, off_mask, off_tiles, own, arr0, arr1, arr2, diag_stored,
    keep, out1, out2, out3, acc, diag_tiles, sem,
):
    load = pltpu.make_async_copy(diag_stored, diag_tiles, sem)
    load.start()
    strips, _, size, _ = diag_tiles.shape
    shift = strips * lax.axis_index("qtr")
    acc[...] = jnp.zeros_like(acc)
    for partner, arrived in enumerate((arr0, arr1, arr2)):
        for strip in range(strips):
            rows = pl.ds(strip * size, size)
            spread_add(
                acc, off_tiles.at[partner, strip], lambda i: off_mask[partner, strip, i],
                lambda i: off_rows[partner, strip, i], False, arrived[rows, :], shift,
            )
    load.wait()
    for strip in range(strips):
        rows = pl.ds(strip * size, size)
        spread_add(
            acc, diag_tiles.at[strip], lambda i: diag_mask[strip, i], lambda i: diag_cols[strip, i],
            True, own[rows, :], shift,
        )
    span = strips * size
    keep[...] = acc[0:span, :]
    for part, out in enumerate((out1, out2, out3)):
        out[...] = acc[(part + 1) * span:(part + 2) * span, :].astype(jnp.bfloat16)


def collect(parts, gathered):
    span = parts[0].shape[0]
    for i, part in enumerate(parts):
        gathered[i * span:(i + 1) * span, :] = part[...]


def partner_kernel(off_rows, off_mask, off_tiles, part0, part1, part2, part3, out0, out1, out2, gathered):
    strips, slots, size, _ = off_tiles.shape[1:]
    shift = strips * lax.axis_index("qtr")
    collect((part0, part1, part2, part3), gathered)
    for partner, out in ((2, out2), (1, out1), (0, out0)):
        for strip in range(strips):
            total = None
            for slot in range(slots):
                place = pl.multiple_of((off_rows[partner, strip, slot] ^ shift) * size, size)
                tile = live(off_tiles[partner, strip, slot], off_mask[partner, strip, slot])
                term = dot_flipped(tile, gathered[pl.ds(place, size), :])
                total = term if total is None else total + term
            out[strip * size:(strip + 1) * size, :] = total.astype(out.dtype)


def base_kernel(
    diag_cols, diag_mask, diag_tiles, part0, part1, part2, part3, keep, vectors, previous, base, gathered,
):
    strips, slots, size, _ = diag_tiles.shape
    shift = strips * lax.axis_index("qtr")
    collect((part0, part1, part2, part3), gathered)
    for strip in range(strips):
        rows = pl.ds(strip * size, size)
        total = keep[rows, :]
        for slot in range(slots):
            place = pl.multiple_of((diag_cols[strip, slot] ^ shift) * size, size)
            tile = live(diag_tiles[strip, slot], diag_mask[strip, slot])
            total = total + dot_plain(tile, gathered[pl.ds(place, size), :])
        base[rows, :] = 2.0 / cheb_half * (total - cheb_center * vectors[rows, :]) - previous[rows, :]


smem = pl.BlockSpec(memory_space=pltpu.SMEM)
vmem = pl.BlockSpec(memory_space=pltpu.VMEM)
anywhere = pl.BlockSpec(memory_space=pl.ANY)


def near(x):
    return pltpu.with_memory_space_constraint(x, pltpu.VMEM)


def far(x):
    return pltpu.with_memory_space_constraint(x, pltpu.HBM)


def call(kernel, scalars, arrays, outs, scratch, stored=()):
    return pl.pallas_call(
        kernel,
        in_specs=[smem] * len(scalars) + [vmem] * len(arrays) + [anywhere] * len(stored),
        out_specs=[vmem] * len(outs),
        out_shape=[pltpu.VMEM(shape, dtype) for shape, dtype in outs],
        scratch_shapes=scratch,
        compiler_params=pltpu.CompilerParams(vmem_limit_bytes=24 << 20),
    )(*[far(x) for x in scalars], *[near(x) for x in arrays], *[far(x) for x in stored])


def on_device(vectors, previous, diag_tiles, diag_cols, diag_mask, off_tiles, off_rows, off_mask):
    rows, width = vectors.shape
    quarters = lax.axis_size("qtr")
    levels = lax.axis_size("grp").bit_length() - 1
    bits = [1 << 0, 1 << levels // 2, 1 << levels - 1]
    half = ((rows, width), jnp.bfloat16)
    full = ((rows, width), jnp.float32)
    group_half = pltpu.VMEM((quarters * rows, width), jnp.bfloat16)
    group_full = pltpu.VMEM((quarters * rows, width), jnp.float32)

    own = vectors.astype(jnp.bfloat16)
    part2 = swap(own, "qtr", 2)
    arr2 = swap(own, "grp", bits[2])
    part1 = swap(own, "qtr", 1)
    arr1 = swap(own, "grp", bits[1])
    arr0 = swap(own, "grp", bits[0])
    part3 = swap(part2, "qtr", 1)

    keep, send1, send2, send3 = call(
        scatter_kernel, (diag_cols, diag_mask, off_rows, off_mask),
        (off_tiles, own, arr0, arr1, arr2), (full, half, half, half),
        [group_full, pltpu.VMEM(diag_tiles.shape, jnp.bfloat16), pltpu.SemaphoreType.DMA], (diag_tiles,),
    )
    got3 = swap(send3, "qtr", 3)
    got2 = swap(send2, "qtr", 2)
    got1 = swap(send1, "qtr", 1)

    parts = (own, part1, part2, part3)
    away0, away1, away2 = call(
        partner_kernel, (off_rows, off_mask), (off_tiles, *parts),
        (half, half, half), [group_half],
    )
    back2 = swap(away2, "grp", bits[2])
    back1 = swap(away1, "grp", bits[1])
    back0 = swap(away0, "grp", bits[0])
    (base,) = call(
        base_kernel, (diag_cols, diag_mask),
        (diag_tiles, *parts, keep, vectors, previous), (full,), [group_half],
    )

    total = base
    for term in (back0, back1, got1, got3, got2, back2):
        total = total + 2.0 / cheb_half * term.astype(jnp.float32)
    return total


def solution(mesh):
    spread = P(("grp", "qtr"))
    spread_off = P(None, ("grp", "qtr"))
    in_specs = (spread,) * 5 + (spread_off,) * 3
    return jax.shard_map(
        on_device, mesh=mesh, in_specs=in_specs, out_specs=spread, check_vma=False
    )
```

profile of v0, /device:TPU:1, one launch (start us, length us, event | category | flops | bytes accessed | tf_op | source)
XLA Modules:
  0.0 70.6 jit_solution(13571326156626293961)
XLA Ops:
  0.0 1.1 %convert_element_type.21.own.part0 = bf16[256,512]{1,0:T(8,128)(2,1)S(1)} convert(f32[256,512]{1,0:T(8,128)} %vectors.1) | non-fusion elementwise | flops 131072 | bytes 786432 | tf_op jit(solution)/shard_map/convert_element_type | solution.py:139
  1.2 6.6 %collective-permute-start.1 = (bf16[256,512]{1,0:T(8,128)(2,1)S(1)}, bf16[256,512]{1,0:T(8,128)(2,1)S(1)}, u32[]{:S(2)}, u32[]{:S(2)}) collective-permute-start(bf16[256,512]{1,0:T(8,128)(2,1)S(1)} %convert_element_type.21.own.part0), channel_id=1, source_target_pairs={{0,2},{1,3},{2,0},{3,1},{4,6},{5,7},{6,4},{7,5},{8,10},{9,11},{10,... | collective-permute-start | bytes 786440 | tf_op jit(solution)/shard_map/ppermute | solution.py:15
  7.8 7.5 %collective-permute-start.5 = (bf16[256,512]{1,0:T(8,128)(2,1)S(1)}, bf16[256,512]{1,0:T(8,128)(2,1)S(1)}, u32[]{:S(2)}, u32[]{:S(2)}) collective-permute-start(bf16[256,512]{1,0:T(8,128)(2,1)S(1)} %convert_element_type.21.own.part0), channel_id=1, source_target_pairs={{0,256},{4,260},{8,264},{12,268},{16,272},{20,276},{24,280},{28,28... | collective-permute-start | bytes 786440 | tf_op jit(solution)/shard_map/ppermute | solution.py:15
  15.2 4.7 %collective-permute-start.4 = (bf16[256,512]{1,0:T(8,128)(2,1)S(1)}, bf16[256,512]{1,0:T(8,128)(2,1)S(1)}, u32[]{:S(2)}, u32[]{:S(2)}) collective-permute-start(bf16[256,512]{1,0:T(8,128)(2,1)S(1)} %convert_element_type.21.own.part0), channel_id=1, source_target_pairs={{0,32},{4,36},{8,40},{12,44},{16,48},{20,52},{24,56},{28,60},{32,0... | collective-permute-start | bytes 786440 | tf_op jit(solution)/shard_map/ppermute | solution.py:15
  19.9 3.4 %collective-permute-start.3 = (bf16[256,512]{1,0:T(8,128)(2,1)S(1)}, bf16[256,512]{1,0:T(8,128)(2,1)S(1)}, u32[]{:S(2)}, u32[]{:S(2)}) collective-permute-start(bf16[256,512]{1,0:T(8,128)(2,1)S(1)} %convert_element_type.21.own.part0), channel_id=1, source_target_pairs={{0,4},{4,0},{8,12},{12,8},{16,20},{20,16},{24,28},{28,24},{32,36},... | collective-permute-start | bytes 786440 | tf_op jit(solution)/shard_map/ppermute | solution.py:15
  23.3 4.0 %collective-permute-start = (bf16[256,512]{1,0:T(8,128)(2,1)S(1)}, bf16[256,512]{1,0:T(8,128)(2,1)S(1)}, u32[]{:S(2)}, u32[]{:S(2)}) collective-permute-start(bf16[256,512]{1,0:T(8,128)(2,1)S(1)} %convert_element_type.21.own.part0), channel_id=1, source_target_pairs={{0,1},{1,0},{2,3},{3,2},{4,5},{5,4},{6,7},{7,6},{8,9},{9,8},{10,11... | collective-permute-start | bytes 786440 | tf_op jit(solution)/shard_map/ppermute | solution.py:15
  27.3 0.0 collective-permute-done.1.part2
  27.4 1.9 %collective-permute-start.2 = (bf16[256,512]{1,0:T(8,128)(2,1)S(1)}, bf16[256,512]{1,0:T(8,128)(2,1)S(1)}, u32[]{:S(2)}, u32[]{:S(2)}) collective-permute-start(bf16[256,512]{1,0:T(8,128)(2,1)S(1)} %collective-permute-done.1.part2), channel_id=1, source_target_pairs={{0,1},{1,0},{2,3},{3,2},{4,5},{5,4},{6,7},{7,6},{8,9},{9,8},{10,11... | collective-permute-start | bytes 786440 | tf_op jit(solution)/shard_map/ppermute | solution.py:15
  29.3 0.0 collective-permute-done.5.arr2
  29.3 0.0 collective-permute-done.4.arr1
  29.3 0.0 collective-permute-done.3.arr0
  29.3 3.2 %shard_map.82 = (f32[256,512]{1,0:T(8,128)S(1)}, bf16[256,512]{1,0:T(8,128)(2,1)S(1)}, bf16[256,512]{1,0:T(8,128)(2,1)S(1)}, bf16[256,512]{1,0:T(8,128)(2,1)S(1)}) custom-call(s32[2,4]{1,0:T(2,128)} %diag_cols.3, s32[2,4]{1,0:T(2,128)} %diag_mask.3, s32[3,2,4]{2,1,0:T(2,128)} %off_rows.3, s32[3,2,4]{2,1,0:T(2,128)} %off_mask.3, ...), custom_call_target="tpu_custom_call" | custom-call | tf_op jit(solution)/shard_map/pallas_call | solution.py:119
  32.6 3.3 %collective-permute-start.8 = (bf16[256,512]{1,0:T(8,128)(2,1)S(1)}, bf16[256,512]{1,0:T(8,128)(2,1)S(1)}, u32[]{:S(2)}, u32[]{:S(2)}) collective-permute-start(bf16[256,512]{1,0:T(8,128)(2,1)S(1)} %get-tuple-element.15), channel_id=1, source_target_pairs={{0,1},{1,0},{2,3},{3,2},{4,5},{5,4},{6,7},{7,6},{8,9},{9,8},{10,11... | collective-permute-start | bytes 786440 | tf_op jit(solution)/shard_map/ppermute | solution.py:15
  35.9 1.9 %collective-permute-start.9 = (bf16[256,512]{1,0:T(8,128)(2,1)S(1)}, bf16[256,512]{1,0:T(8,128)(2,1)S(1)}, u32[]{:S(2)}, u32[]{:S(2)}) collective-permute-start(bf16[256,512]{1,0:T(8,128)(2,1)S(1)} %get-tuple-element.16), channel_id=1, source_target_pairs={{0,3},{1,2},{2,1},{3,0},{4,7},{5,6},{6,5},{7,4},{8,11},{9,10},{10,... | collective-permute-start | bytes 786440 | tf_op jit(solution)/shard_map/ppermute | solution.py:15
  37.9 0.0 copy-start.1
  37.9 0.0 copy-start.2
  37.9 0.0 copy-start.3
  37.9 3.2 %collective-permute-start.10 = (bf16[256,512]{1,0:T(8,128)(2,1)S(1)}, bf16[256,512]{1,0:T(8,128)(2,1)S(1)}, u32[]{:S(2)}, u32[]{:S(2)}) collective-permute-start(bf16[256,512]{1,0:T(8,128)(2,1)S(1)} %get-tuple-element.17), channel_id=1, source_target_pairs={{0,2},{1,3},{2,0},{3,1},{4,6},{5,7},{6,4},{7,5},{8,10},{9,11},{10,... | collective-permute-start | bytes 786440 | tf_op jit(solution)/shard_map/ppermute | solution.py:15
  41.1 0.0 collective-permute-done.part1
  41.2 0.0 collective-permute-done.2.part3
  41.2 1.8 %shard_map.84 = (bf16[256,512]{1,0:T(8,128)(2,1)S(1)}, bf16[256,512]{1,0:T(8,128)(2,1)S(1)}, bf16[256,512]{1,0:T(8,128)(2,1)S(1)}) custom-call(s32[3,2,4]{2,1,0:T(2,128)} %off_rows.3, s32[3,2,4]{2,1,0:T(2,128)} %off_mask.3, bf16[3,2,4,128,128]{4,3,2,1,0:T(8,128)(2,1)S(1)} %copy-done, bf16[256,512]{1,0:T(8,128)(2,1)S(1)} %convert_element_type.21.own.part0, ...), custom_call_target="tpu_custom_call" | custom-call | tf_op jit(solution)/shard_map/pallas_call | solution.py:119
  43.0 3.0 %collective-permute-start.6 = (bf16[256,512]{1,0:T(8,128)(2,1)S(1)}, bf16[256,512]{1,0:T(8,128)(2,1)S(1)}, u32[]{:S(2)}, u32[]{:S(2)}) collective-permute-start(bf16[256,512]{1,0:T(8,128)(2,1)S(1)} %get-tuple-element.13), channel_id=1, source_target_pairs={{0,4},{4,0},{8,12},{12,8},{16,20},{20,16},{24,28},{28,24},{32,36},... | collective-permute-start | bytes 786440 | tf_op jit(solution)/shard_map/ppermute | solution.py:15
  46.0 2.7 %collective-permute-start.7 = (bf16[256,512]{1,0:T(8,128)(2,1)S(1)}, bf16[256,512]{1,0:T(8,128)(2,1)S(1)}, u32[]{:S(2)}, u32[]{:S(2)}) collective-permute-start(bf16[256,512]{1,0:T(8,128)(2,1)S(1)} %get-tuple-element.14), channel_id=1, source_target_pairs={{0,32},{4,36},{8,40},{12,44},{16,48},{20,52},{24,56},{28,60},{32,0... | collective-permute-start | bytes 786440 | tf_op jit(solution)/shard_map/ppermute | solution.py:15
  48.8 2.1 %collective-permute-done.8 = bf16[256,512]{1,0:T(8,128)(2,1)S(1)} collective-permute-done((bf16[256,512]{1,0:T(8,128)(2,1)S(1)}, bf16[256,512]{1,0:T(8,128)(2,1)S(1)}, u32[]{:S(2)}, u32[]{:S(2)}) %collective-permute-start.8) | collective-permute-done | bytes 262176 | tf_op jit(solution)/shard_map/ppermute | solution.py:15
  50.9 5.9 %collective-permute-start.11 = (bf16[256,512]{1,0:T(8,128)(2,1)S(1)}, bf16[256,512]{1,0:T(8,128)(2,1)S(1)}, u32[]{:S(2)}, u32[]{:S(2)}) collective-permute-start(bf16[256,512]{1,0:T(8,128)(2,1)S(1)} %get-tuple-element.18), channel_id=1, source_target_pairs={{0,256},{4,260},{8,264},{12,268},{16,272},{20,276},{24,280},{28,28... | collective-permute-start | bytes 786440 | tf_op jit(solution)/shard_map/ppermute | solution.py:15
  56.9 1.2 %shard_map.83 = f32[256,512]{1,0:T(8,128)S(1)} custom-call(s32[2,4]{1,0:T(2,128)} %diag_cols.3, s32[2,4]{1,0:T(2,128)} %diag_mask.3, bf16[2,4,128,128]{3,2,1,0:T(8,128)(2,1)S(1)} %copy-done.2, bf16[256,512]{1,0:T(8,128)(2,1)S(1)} %convert_element_type.21.own.part0, bf16[256,512]{1,0:T(8,128)(2,1)S(1)} %collective-permute-done.part1, ...), custom_call_target="tpu_custom_call" | custom-call | tf_op jit(solution)/shard_map/pallas_call | solution.py:119
  58.1 0.0 collective-permute-done.9
  58.1 3.6 %collective-permute-done.10 = bf16[256,512]{1,0:T(8,128)(2,1)S(1)} collective-permute-done((bf16[256,512]{1,0:T(8,128)(2,1)S(1)}, bf16[256,512]{1,0:T(8,128)(2,1)S(1)}, u32[]{:S(2)}, u32[]{:S(2)}) %collective-permute-start.10) | collective-permute-done | bytes 262176 | tf_op jit(solution)/shard_map/ppermute | solution.py:15
  61.7 0.0 collective-permute-done.6
  61.7 0.0 collective-permute-done.7
  61.7 7.9 %collective-permute-done.11 = bf16[256,512]{1,0:T(8,128)(2,1)S(1)} collective-permute-done((bf16[256,512]{1,0:T(8,128)(2,1)S(1)}, bf16[256,512]{1,0:T(8,128)(2,1)S(1)}, u32[]{:S(2)}, u32[]{:S(2)}) %collective-permute-start.11) | collective-permute-done | bytes 262176 | tf_op jit(solution)/shard_map/ppermute | solution.py:15
  69.6 1.0 %convert_add_fusion = f32[256,512]{1,0:T(8,128)} fusion(bf16[256,512]{1,0:T(8,128)(2,1)S(1)} %collective-permute-done.11, bf16[256,512]{1,0:T(8,128)(2,1)S(1)} %collective-permute-done.10, bf16[256,512]{1,0:T(8,128)(2,1)S(1)} %collective-permute-done.9, bf16[256,512]{1,0:T(8,128)(2,1)S(1)} %collective-permute-done.8, ...), kind=kLoop, calls=%fused_computation | loop fusion | flops 1572864 | bytes 2621440 | tf_op jit(solution)/shard_map/add | solution.py:171
  (5 shorter events, 0.0 us)
Async XLA Ops:
  0.0 29.3 %copy-start = (bf16[3,2,4,128,128]{4,3,2,1,0:T(8,128)(2,1)S(1)}, bf16[3,2,4,128,128]{4,3,2,1,0:T(8,128)(2,1)}, u32[]{:S(2)}) copy-start(bf16[3,2,4,128,128]{4,3,2,1,0:T(8,128)(2,1)} %off_tiles.3) | copy-start | bytes 2359300
  1.2 26.2 %collective-permute-start.1 = (bf16[256,512]{1,0:T(8,128)(2,1)S(1)}, bf16[256,512]{1,0:T(8,128)(2,1)S(1)}, u32[]{:S(2)}, u32[]{:S(2)}) collective-permute-start(bf16[256,512]{1,0:T(8,128)(2,1)S(1)} %convert_element_type.21.own.part0), channel_id=1, source_target_pairs={{0,2},{1,3},{2,0},{3,1},{4,6},{5,7},{6,4},{7,5},{8,10},{9,11},{10,... | collective-permute-start | bytes 786440 | tf_op jit(solution)/shard_map/ppermute | solution.py:15
  7.8 21.5 %collective-permute-start.5 = (bf16[256,512]{1,0:T(8,128)(2,1)S(1)}, bf16[256,512]{1,0:T(8,128)(2,1)S(1)}, u32[]{:S(2)}, u32[]{:S(2)}) collective-permute-start(bf16[256,512]{1,0:T(8,128)(2,1)S(1)} %convert_element_type.21.own.part0), channel_id=1, source_target_pairs={{0,256},{4,260},{8,264},{12,268},{16,272},{20,276},{24,280},{28,28... | collective-permute-start | bytes 786440 | tf_op jit(solution)/shard_map/ppermute | solution.py:15
  15.2 14.1 %collective-permute-start.4 = (bf16[256,512]{1,0:T(8,128)(2,1)S(1)}, bf16[256,512]{1,0:T(8,128)(2,1)S(1)}, u32[]{:S(2)}, u32[]{:S(2)}) collective-permute-start(bf16[256,512]{1,0:T(8,128)(2,1)S(1)} %convert_element_type.21.own.part0), channel_id=1, source_target_pairs={{0,32},{4,36},{8,40},{12,44},{16,48},{20,52},{24,56},{28,60},{32,0... | collective-permute-start | bytes 786440 | tf_op jit(solution)/shard_map/ppermute | solution.py:15
  19.9 9.4 %collective-permute-start.3 = (bf16[256,512]{1,0:T(8,128)(2,1)S(1)}, bf16[256,512]{1,0:T(8,128)(2,1)S(1)}, u32[]{:S(2)}, u32[]{:S(2)}) collective-permute-start(bf16[256,512]{1,0:T(8,128)(2,1)S(1)} %convert_element_type.21.own.part0), channel_id=1, source_target_pairs={{0,4},{4,0},{8,12},{12,8},{16,20},{20,16},{24,28},{28,24},{32,36},... | collective-permute-start | bytes 786440 | tf_op jit(solution)/shard_map/ppermute | solution.py:15
  23.3 17.8 %collective-permute-start = (bf16[256,512]{1,0:T(8,128)(2,1)S(1)}, bf16[256,512]{1,0:T(8,128)(2,1)S(1)}, u32[]{:S(2)}, u32[]{:S(2)}) collective-permute-start(bf16[256,512]{1,0:T(8,128)(2,1)S(1)} %convert_element_type.21.own.part0), channel_id=1, source_target_pairs={{0,1},{1,0},{2,3},{3,2},{4,5},{5,4},{6,7},{7,6},{8,9},{9,8},{10,11... | collective-permute-start | bytes 786440 | tf_op jit(solution)/shard_map/ppermute | solution.py:15
  27.4 13.8 %collective-permute-start.2 = (bf16[256,512]{1,0:T(8,128)(2,1)S(1)}, bf16[256,512]{1,0:T(8,128)(2,1)S(1)}, u32[]{:S(2)}, u32[]{:S(2)}) collective-permute-start(bf16[256,512]{1,0:T(8,128)(2,1)S(1)} %collective-permute-done.1.part2), channel_id=1, source_target_pairs={{0,1},{1,0},{2,3},{3,2},{4,5},{5,4},{6,7},{7,6},{8,9},{9,8},{10,11... | collective-permute-start | bytes 786440 | tf_op jit(solution)/shard_map/ppermute | solution.py:15
  32.6 18.3 %collective-permute-start.8 = (bf16[256,512]{1,0:T(8,128)(2,1)S(1)}, bf16[256,512]{1,0:T(8,128)(2,1)S(1)}, u32[]{:S(2)}, u32[]{:S(2)}) collective-permute-start(bf16[256,512]{1,0:T(8,128)(2,1)S(1)} %get-tuple-element.15), channel_id=1, source_target_pairs={{0,1},{1,0},{2,3},{3,2},{4,5},{5,4},{6,7},{7,6},{8,9},{9,8},{10,11... | collective-permute-start | bytes 786440 | tf_op jit(solution)/shard_map/ppermute | solution.py:15
  35.9 22.2 %collective-permute-start.9 = (bf16[256,512]{1,0:T(8,128)(2,1)S(1)}, bf16[256,512]{1,0:T(8,128)(2,1)S(1)}, u32[]{:S(2)}, u32[]{:S(2)}) collective-permute-start(bf16[256,512]{1,0:T(8,128)(2,1)S(1)} %get-tuple-element.16), channel_id=1, source_target_pairs={{0,3},{1,2},{2,1},{3,0},{4,7},{5,6},{6,5},{7,4},{8,11},{9,10},{10,... | collective-permute-start | bytes 786440 | tf_op jit(solution)/shard_map/ppermute | solution.py:15
  37.9 19.0 %copy-start.1 = (f32[256,512]{1,0:T(8,128)S(1)}, f32[256,512]{1,0:T(8,128)}, u32[]{:S(2)}) copy-start(f32[256,512]{1,0:T(8,128)} %vectors.1) | copy-start | bytes 1572868
  37.9 19.0 %copy-start.2 = (bf16[2,4,128,128]{3,2,1,0:T(8,128)(2,1)S(1)}, bf16[2,4,128,128]{3,2,1,0:T(8,128)(2,1)}, u32[]{:S(2)}) copy-start(bf16[2,4,128,128]{3,2,1,0:T(8,128)(2,1)} %diag_tiles.1) | copy-start | bytes 786436
  37.9 19.0 %copy-start.3 = (f32[256,512]{1,0:T(8,128)S(1)}, f32[256,512]{1,0:T(8,128)}, u32[]{:S(2)}) copy-start(f32[256,512]{1,0:T(8,128)} %previous.1) | copy-start | bytes 1572868
  37.9 23.8 %collective-permute-start.10 = (bf16[256,512]{1,0:T(8,128)(2,1)S(1)}, bf16[256,512]{1,0:T(8,128)(2,1)S(1)}, u32[]{:S(2)}, u32[]{:S(2)}) collective-permute-start(bf16[256,512]{1,0:T(8,128)(2,1)S(1)} %get-tuple-element.17), channel_id=1, source_target_pairs={{0,2},{1,3},{2,0},{3,1},{4,6},{5,7},{6,4},{7,5},{8,10},{9,11},{10,... | collective-permute-start | bytes 786440 | tf_op jit(solution)/shard_map/ppermute | solution.py:15
  43.0 18.7 %collective-permute-start.6 = (bf16[256,512]{1,0:T(8,128)(2,1)S(1)}, bf16[256,512]{1,0:T(8,128)(2,1)S(1)}, u32[]{:S(2)}, u32[]{:S(2)}) collective-permute-start(bf16[256,512]{1,0:T(8,128)(2,1)S(1)} %get-tuple-element.13), channel_id=1, source_target_pairs={{0,4},{4,0},{8,12},{12,8},{16,20},{20,16},{24,28},{28,24},{32,36},... | collective-permute-start | bytes 786440 | tf_op jit(solution)/shard_map/ppermute | solution.py:15
  46.0 15.7 %collective-permute-start.7 = (bf16[256,512]{1,0:T(8,128)(2,1)S(1)}, bf16[256,512]{1,0:T(8,128)(2,1)S(1)}, u32[]{:S(2)}, u32[]{:S(2)}) collective-permute-start(bf16[256,512]{1,0:T(8,128)(2,1)S(1)} %get-tuple-element.14), channel_id=1, source_target_pairs={{0,32},{4,36},{8,40},{12,44},{16,48},{20,52},{24,56},{28,60},{32,0... | collective-permute-start | bytes 786440 | tf_op jit(solution)/shard_map/ppermute | solution.py:15
  50.9 18.7 %collective-permute-start.11 = (bf16[256,512]{1,0:T(8,128)(2,1)S(1)}, bf16[256,512]{1,0:T(8,128)(2,1)S(1)}, u32[]{:S(2)}, u32[]{:S(2)}) collective-permute-start(bf16[256,512]{1,0:T(8,128)(2,1)S(1)} %get-tuple-element.18), channel_id=1, source_target_pairs={{0,256},{4,260},{8,264},{12,268},{16,272},{20,276},{24,280},{28,28... | collective-permute-start | bytes 786440 | tf_op jit(solution)/shard_map/ppermute | solution.py:15
where the time goes:
time: 71.2 us; the launch traced here: 70.6 us
  starting transfers between devices  48.3 us (68%)
  waiting for transfers between devices  13.6 us (19%)
  Pallas kernels  6.25 us (9%)
  other arithmetic  2.17 us (3%)
    ppermute x12, starting transfers between devices, swap(): return lax.ppermute(block, axis, [(i, i ^ mask) for i in range(count)])  48.3 us
    ppermute x12, waiting for transfers between devices, swap(): return lax.ppermute(block, axis, [(i, i ^ mask) for i in range(count)])  13.6 us
    pallas_call x3, Pallas kernels, call(): pl.pallas_call(kernel, in_specs=[smem] * len(scalars) + [vmem] * len(arra...  6.25 us
  transfers between devices with their start and end apart: 12, of which 3 were waited for; matrix products, arithmetic and copies ran while one was open for 0% of the time, Pallas kernels for 9%

commit v1 on v0

v1 whole, which is shorter than its diff:
```python
import jax
import jax.numpy as jnp
from jax import lax
from jax.experimental import pallas as pl
from jax.experimental.pallas import tpu as pltpu
from jax.sharding import PartitionSpec as P


cheb_center = 0.25
cheb_half = 2.0


def swap(block, axis, mask):
    count = lax.axis_size(axis)
    return lax.ppermute(block, axis, [(i, i ^ mask) for i in range(count)])


def live(tile, flag):
    return (tile.astype(jnp.float32) * flag.astype(jnp.float32)).astype(jnp.bfloat16)


def dot_plain(a, b):
    return lax.dot_general(a, b, (((1,), (0,)), ((), ())), preferred_element_type=jnp.float32)


def dot_flipped(a, b):
    return lax.dot_general(a, b, (((0,), (0,)), ((), ())), preferred_element_type=jnp.float32)


def spread_add(acc, tiles, flags, places, flipped, block, shift):
    slots, size, _ = tiles.shape
    for slot in range(slots):
        place = pl.multiple_of((places(slot) ^ shift) * size, size)
        tile = live(tiles[slot], flags(slot))
        product = dot_flipped(tile, block) if flipped else dot_plain(tile, block)
        acc[pl.ds(place, size), :] += product


def load_kernel(vectors, *refs):
    staged, sems = refs[-2:]
    count = len(refs) // 2 - 1
    own = refs[count]
    chunks = sems.shape[0] - count
    span = vectors.shape[0] // chunks
    pieces = [pl.ds(i * span, span) for i in range(chunks)]
    copies = [
        pltpu.make_async_copy(vectors.at[rows, :], staged.at[rows, :], sems.at[i])
        for i, rows in enumerate(pieces)
    ]
    copies += [
        pltpu.make_async_copy(refs[i], refs[count + 1 + i], sems.at[chunks + i]) for i in range(count)
    ]
    for copy in copies:
        copy.start()
    for copy, rows in zip(copies, pieces):
        copy.wait()
        own[rows, :] = staged[rows, :].astype(jnp.bfloat16)
    for copy in copies[chunks:]:
        copy.wait()


def partner_spread(acc, partners, arrivals, off_rows, off_mask, off_tiles, shift):
    strips, _, size, _ = off_tiles.shape[1:]
    for partner, arrived in zip(partners, arrivals):
        for strip in range(strips):
            spread_add(
                acc, off_tiles.at[partner, strip], lambda i: off_mask[partner, strip, i],
                lambda i: off_rows[partner, strip, i], False, arrived[strip * size:(strip + 1) * size, :], shift,
            )


def early_kernel(diag_cols, diag_mask, off_rows, off_mask, diag_tiles, off_tiles, own, arr0, arr1, acc):
    strips, _, size, _ = diag_tiles.shape
    shift = strips * lax.axis_index("qtr")
    acc[...] = jnp.zeros_like(acc)
    for strip in range(strips):
        spread_add(
            acc, diag_tiles.at[strip], lambda i: diag_mask[strip, i], lambda i: diag_cols[strip, i],
            True, own[strip * size:(strip + 1) * size, :], shift,
        )
    partner_spread(acc, (0, 1), (arr0, arr1), off_rows, off_mask, off_tiles, shift)


def late_kernel(off_rows, off_mask, off_tiles, arr2, before, acc, out1, out3):
    strips, _, size, _ = off_tiles.shape[1:]
    shift = strips * lax.axis_index("qtr")
    partner_spread(acc, (2,), (arr2,), off_rows, off_mask, off_tiles, shift)
    span = strips * size
    out1[...] = acc[span:2 * span, :].astype(jnp.bfloat16)
    out3[...] = acc[3 * span:, :].astype(jnp.bfloat16)


def collect(parts, gathered):
    span = parts[0].shape[0]
    for i, part in enumerate(parts):
        gathered[i * span:(i + 1) * span, :] = part[...]


def partner_products(partner, out, off_rows, off_mask, off_tiles, gathered, shift):
    strips, slots, size, _ = off_tiles.shape[1:]
    for strip in range(strips):
        total = None
        for slot in range(slots):
            place = pl.multiple_of((off_rows[partner, strip, slot] ^ shift) * size, size)
            tile = live(off_tiles[partner, strip, slot], off_mask[partner, strip, slot])
            term = dot_flipped(tile, gathered[pl.ds(place, size), :])
            total = term if total is None else total + term
        out[strip * size:(strip + 1) * size, :] = total.astype(out.dtype)


def outer_kernel(off_rows, off_mask, off_tiles, part0, part1, part2, part3, gathered, out2, out1):
    shift = off_tiles.shape[1] * lax.axis_index("qtr")
    collect((part0, part1, part2, part3), gathered)
    partner_products(2, out2, off_rows, off_mask, off_tiles, gathered, shift)
    partner_products(1, out1, off_rows, off_mask, off_tiles, gathered, shift)


def inner_kernel(off_rows, off_mask, off_tiles, gathered, out0):
    shift = off_tiles.shape[1] * lax.axis_index("qtr")
    partner_products(0, out0, off_rows, off_mask, off_tiles, gathered, shift)


def base_kernel(diag_cols, diag_mask, diag_tiles, gathered, acc, got1, vectors, previous, base):
    strips, slots, size, _ = diag_tiles.shape
    shift = strips * lax.axis_index("qtr")
    for strip in range(strips):
        rows = pl.ds(strip * size, size)
        total = acc[rows, :] + got1[rows, :].astype(jnp.float32)
        for slot in range(slots):
            place = pl.multiple_of((diag_cols[strip, slot] ^ shift) * size, size)
            tile = live(diag_tiles[strip, slot], diag_mask[strip, slot])
            total = total + dot_plain(tile, gathered[pl.ds(place, size), :])
        base[rows, :] = 2.0 / cheb_half * (total - cheb_center * vectors[rows, :]) - previous[rows, :]


smem = pl.BlockSpec(memory_space=pltpu.SMEM)
vmem = pl.BlockSpec(memory_space=pltpu.VMEM)
anywhere = pl.BlockSpec(memory_space=pl.ANY)


def near(x):
    return pltpu.with_memory_space_constraint(x, pltpu.VMEM)


def far(x):
    return pltpu.with_memory_space_constraint(x, pltpu.HBM)


def call(kernel, scalars, arrays, outs, scratch, stored=(), aliases={}):
    return pl.pallas_call(
        kernel,
        in_specs=[smem] * len(scalars) + [vmem] * len(arrays) + [anywhere] * len(stored),
        out_specs=[vmem] * len(outs),
        out_shape=[pltpu.VMEM(shape, dtype) for shape, dtype in outs],
        scratch_shapes=scratch,
        input_output_aliases=aliases,
        compiler_params=pltpu.CompilerParams(vmem_limit_bytes=24 << 20),
    )(*[near(x) for x in scalars], *[near(x) for x in arrays], *[far(x) for x in stored])


def on_device(vectors, previous, diag_tiles, diag_cols, diag_mask, off_tiles, off_rows, off_mask):
    rows, width = vectors.shape
    quarters = lax.axis_size("qtr")
    levels = lax.axis_size("grp").bit_length() - 1
    bits = [1 << 0, 1 << levels // 2, 1 << levels - 1]
    half = ((rows, width), jnp.bfloat16)
    full = ((rows, width), jnp.float32)
    group_half = ((quarters * rows, width), jnp.bfloat16)
    group_full = ((quarters * rows, width), jnp.float32)

    stored = (diag_tiles, off_tiles, diag_cols, diag_mask, off_rows, off_mask)
    own, diag_tiles, off_tiles, diag_cols, diag_mask, off_rows, off_mask = call(
        load_kernel, (), (), (half, *[(x.shape, x.dtype) for x in stored]),
        [pltpu.VMEM((rows, width), jnp.float32), pltpu.SemaphoreType.DMA((4 + len(stored),))],
        (vectors, *stored),
    )
    part2 = swap(own, "qtr", 2)
    arr2 = swap(own, "grp", bits[2])
    part1 = swap(own, "qtr", 1)
    arr1 = swap(own, "grp", bits[1])
    arr0 = swap(own, "grp", bits[0])
    part3 = swap(part2, "qtr", 1)

    (acc,) = call(
        early_kernel, (diag_cols, diag_mask, off_rows, off_mask),
        (diag_tiles, off_tiles, own, arr0, arr1), (group_full,), [],
    )
    acc, send1, send3 = call(
        late_kernel, (off_rows, off_mask), (off_tiles, arr2, acc),
        (group_full, half, half), [], aliases={4: 0},
    )
    got3 = swap(send3, "qtr", 1)
    send2 = (acc[2 * rows:3 * rows] + got3.astype(jnp.float32)).astype(jnp.bfloat16)
    got2 = swap(send2, "qtr", 2)
    got1 = swap(send1, "qtr", 1)

    parts = (own, part1, part2, part3)
    gathered, away2, away1 = call(
        outer_kernel, (off_rows, off_mask), (off_tiles, *parts),
        (group_half, half, half), [],
    )
    back2 = swap(away2, "grp", bits[2])
    back1 = swap(away1, "grp", bits[1])
    (away0,) = call(inner_kernel, (off_rows, off_mask), (off_tiles, gathered), (half,), [])
    back0 = swap(away0, "grp", bits[0])
    (base,) = call(
        base_kernel, (diag_cols, diag_mask),
        (diag_tiles, gathered, acc, got1, vectors, previous), (full,), [],
    )

    total = base
    for term in (back0, back1, got2, back2):
        total = total + 2.0 / cheb_half * term.astype(jnp.float32)
    return total


def solution(mesh):
    spread = P(("grp", "qtr"))
    spread_off = P(None, ("grp", "qtr"))
    in_specs = (spread,) * 5 + (spread_off,) * 3
    return jax.shard_map(
        on_device, mesh=mesh, in_specs=in_specs, out_specs=spread, check_vma=False
    )
```

time: 71.2 us -> 86.6 us (1.22)
  waiting for transfers between devices: 13.6 us -> 30.6 us
  starting transfers between devices: 48.3 us -> 46.3 us
  Pallas kernels: 6.25 us -> 7.98 us
  other arithmetic: 2.17 us -> 1.03 us
    ppermute x12, waiting for transfers between devices: 13.6 us -> 30.6 us  [swap(): return lax.ppermute(block, axis, [(i, i ^ mask) for i in range(count)])]
    ppermute x12, starting transfers between devices: 48.3 us -> 46.3 us  [swap(): return lax.ppermute(block, axis, [(i, i ^ mask) for i in range(count)])]
    pallas_call x3 -> x6, Pallas kernels: 6.25 us -> 7.98 us  [call(): pl.pallas_call(kernel, in_specs=[smem] * len(scalars) + [vmem] * len(arra...]
    convert_element_type x1, other arithmetic: 1.15 us -> 0.07 us  [on_device(): (acc[2 * rows:3 * rows] + got3.astype(jnp.float32)).astype(jnp.bfloat16)]
  transfers between devices with their start and end apart: 12 -> 12, of which waited for: 3 -> 4; matrix products, arithmetic and copies ran while one was open for 0% -> 0% of each run, Pallas kernels for 9% -> 7%
where the time goes in v1:
time: 86.6 us; the launch traced here: 86.1 us
  starting transfers between devices  46.3 us (53%)
  waiting for transfers between devices  30.6 us (35%)
  Pallas kernels  7.98 us (9%)
  other arithmetic  1.03 us (1%)
    ppermute x12, starting transfers between devices, swap(): return lax.ppermute(block, axis, [(i, i ^ mask) for i in range(count)])  46.3 us
    ppermute x12, waiting for transfers between devices, swap(): return lax.ppermute(block, axis, [(i, i ^ mask) for i in range(count)])  30.6 us
    pallas_call x6, Pallas kernels, call(): pl.pallas_call(kernel, in_specs=[smem] * len(scalars) + [vmem] * len(arra...  7.98 us
  transfers between devices with their start and end apart: 12, of which 4 were waited for; matrix products, arithmetic and copies ran while one was open for 0% of the time, Pallas kernels for 7%

profile of v1, /device:TPU:1, one launch (start us, length us, event | category | flops | bytes accessed | tf_op | source)
XLA Modules:
  0.0 86.1 jit_solution(11424268791104395794)
XLA Ops:
  0.0 1.6 %shard_map.82 = (bf16[256,512]{1,0:T(8,128)(2,1)S(1)}, bf16[2,4,128,128]{3,2,1,0:T(8,128)(2,1)S(1)}, bf16[3,2,4,128,128]{4,3,2,1,0:T(8,128)(2,1)S(1)}, s32[2,4]{...) custom-call(f32[256,512]{1,0:T(8,128)} %vectors.3, ...), custom_call_target="tpu_custom_call" | custom-call | tf_op jit(solution)/shard_map/pallas_call | solution.py:150
  1.6 8.7 %collective-permute-start.4 = (bf16[256,512]{1,0:T(8,128)(2,1)S(1)}, bf16[256,512]{1,0:T(8,128)(2,1)S(1)}, u32[]{:S(2)}, u32[]{:S(2)}) collective-permute-start(bf16[256,512]{1,0:T(8,128)(2,1)S(1)} %get-tuple-element.24.part0.own), channel_id=1, source_target_pairs={{0,4},{4,0},{8,12},{12,8},{16,20},{20,16},{24,28},{28,24},{32,36},... | collective-permute-start | bytes 786440 | tf_op jit(solution)/shard_map/ppermute | solution.py:15
  10.3 1.9 %collective-permute-start.5 = (bf16[256,512]{1,0:T(8,128)(2,1)S(1)}, bf16[256,512]{1,0:T(8,128)(2,1)S(1)}, u32[]{:S(2)}, u32[]{:S(2)}) collective-permute-start(bf16[256,512]{1,0:T(8,128)(2,1)S(1)} %get-tuple-element.24.part0.own), channel_id=1, source_target_pairs={{0,32},{4,36},{8,40},{12,44},{16,48},{20,52},{24,56},{28,60},{32,0... | collective-permute-start | bytes 786440 | tf_op jit(solution)/shard_map/ppermute | solution.py:15
  12.3 4.8 %collective-permute-start.3 = (bf16[256,512]{1,0:T(8,128)(2,1)S(1)}, bf16[256,512]{1,0:T(8,128)(2,1)S(1)}, u32[]{:S(2)}, u32[]{:S(2)}) collective-permute-start(bf16[256,512]{1,0:T(8,128)(2,1)S(1)} %get-tuple-element.24.part0.own), channel_id=1, source_target_pairs={{0,256},{4,260},{8,264},{12,268},{16,272},{20,276},{24,280},{28,28... | collective-permute-start | bytes 786440 | tf_op jit(solution)/shard_map/ppermute | solution.py:15
  17.1 5.8 %collective-permute-start.1 = (bf16[256,512]{1,0:T(8,128)(2,1)S(1)}, bf16[256,512]{1,0:T(8,128)(2,1)S(1)}, u32[]{:S(2)}, u32[]{:S(2)}) collective-permute-start(bf16[256,512]{1,0:T(8,128)(2,1)S(1)} %get-tuple-element.24.part0.own), channel_id=1, source_target_pairs={{0,2},{1,3},{2,0},{3,1},{4,6},{5,7},{6,4},{7,5},{8,10},{9,11},{10,... | collective-permute-start | bytes 786440 | tf_op jit(solution)/shard_map/ppermute | solution.py:15
  22.9 0.0 collective-permute-done.4.arr0
  22.9 0.0 collective-permute-done.5.arr1
  22.9 1.8 %shard_map.84.before = f32[1024,512]{1,0:T(8,128)S(1)} custom-call(s32[2,4]{1,0:T(2,128)S(1)} %get-tuple-element.18.diag_cols, s32[2,4]{1,0:T(2,128)S(1)} %get-tuple-element.19.diag_mask, s32[3,2,4]{2,1,0:T(2,128)S(1)} %get-tuple-element.21.off_rows, s32[3,2,4]{2,1,0:T(2,128)S(1)} %get-tuple-element.22.off_mask, ...), custom_call_target="tpu_custom_call" | custom-call | tf_op jit(solution)/shard_map/pallas_call | solution.py:150
  24.7 6.8 %collective-permute-done.3.arr2 = bf16[256,512]{1,0:T(8,128)(2,1)S(1)} collective-permute-done((bf16[256,512]{1,0:T(8,128)(2,1)S(1)}, bf16[256,512]{1,0:T(8,128)(2,1)S(1)}, u32[]{:S(2)}, u32[]{:S(2)}) %collective-permute-start.3) | collective-permute-done | bytes 262176 | tf_op jit(solution)/shard_map/ppermute | solution.py:15
  31.5 1.1 %shard_map.85 = (f32[1024,512]{1,0:T(8,128)S(1)}, bf16[256,512]{1,0:T(8,128)(2,1)S(1)}, bf16[256,512]{1,0:T(8,128)(2,1)S(1)}) custom-call(s32[3,2,4]{2,1,0:T(2,128)S(1)} %get-tuple-element.21.off_rows, s32[3,2,4]{2,1,0:T(2,128)S(1)} %get-tuple-element.22.off_mask, ...), custom_call_target="tpu_custom_call", output_to_operand_aliasing={{0}: (4, {})} | custom-call | tf_op jit(solution)/shard_map/pallas_call | solution.py:150
  32.6 1.9 %collective-permute-start.9 = (bf16[256,512]{1,0:T(8,128)(2,1)S(1)}, bf16[256,512]{1,0:T(8,128)(2,1)S(1)}, u32[]{:S(2)}, u32[]{:S(2)}) collective-permute-start(bf16[256,512]{1,0:T(8,128)(2,1)S(1)} %get-tuple-element.29), channel_id=1, source_target_pairs={{0,1},{1,0},{2,3},{3,2},{4,5},{5,4},{6,7},{7,6},{8,9},{9,8},{10,11... | collective-permute-start | bytes 786440 | tf_op jit(solution)/shard_map/ppermute | solution.py:15
  34.6 3.4 %collective-permute-start = (bf16[256,512]{1,0:T(8,128)(2,1)S(1)}, bf16[256,512]{1,0:T(8,128)(2,1)S(1)}, u32[]{:S(2)}, u32[]{:S(2)}) collective-permute-start(bf16[256,512]{1,0:T(8,128)(2,1)S(1)} %get-tuple-element.24.part0.own), channel_id=1, source_target_pairs={{0,1},{1,0},{2,3},{3,2},{4,5},{5,4},{6,7},{7,6},{8,9},{9,8},{10,11... | collective-permute-start | bytes 786440 | tf_op jit(solution)/shard_map/ppermute | solution.py:15
  37.9 0.0 collective-permute-done.1.part2
  37.9 1.9 %collective-permute-start.2 = (bf16[256,512]{1,0:T(8,128)(2,1)S(1)}, bf16[256,512]{1,0:T(8,128)(2,1)S(1)}, u32[]{:S(2)}, u32[]{:S(2)}) collective-permute-start(bf16[256,512]{1,0:T(8,128)(2,1)S(1)} %collective-permute-done.1.part2), channel_id=1, source_target_pairs={{0,1},{1,0},{2,3},{3,2},{4,5},{5,4},{6,7},{7,6},{8,9},{9,8},{10,11... | collective-permute-start | bytes 786440 | tf_op jit(solution)/shard_map/ppermute | solution.py:15
  39.9 3.4 %collective-permute-start.6 = (bf16[256,512]{1,0:T(8,128)(2,1)S(1)}, bf16[256,512]{1,0:T(8,128)(2,1)S(1)}, u32[]{:S(2)}, u32[]{:S(2)}) collective-permute-start(bf16[256,512]{1,0:T(8,128)(2,1)S(1)} %get-tuple-element.27), channel_id=1, source_target_pairs={{0,1},{1,0},{2,3},{3,2},{4,5},{5,4},{6,7},{7,6},{8,9},{9,8},{10,11... | collective-permute-start | bytes 786440 | tf_op jit(solution)/shard_map/ppermute | solution.py:15
  43.2 0.0 collective-permute-done.9
  43.3 0.1 add_convert_fusion
  43.3 0.0 copy-start
  43.3 0.0 copy-start.1
  43.4 2.1 %collective-permute-start.10 = (bf16[256,512]{1,0:T(8,128)(2,1)S(1)}, bf16[256,512]{1,0:T(8,128)(2,1)S(1)}, u32[]{:S(2)}, u32[]{:S(2)}) collective-permute-start(bf16[256,512]{1,0:T(8,128)(2,1)S(1)} %add_convert_fusion), channel_id=1, source_target_pairs={{0,2},{1,3},{2,0},{3,1},{4,6},{5,7},{6,4},{7,5},{8,10},{9,11},{10,... | collective-permute-start | bytes 786440 | tf_op jit(solution)/shard_map/ppermute | solution.py:15
  45.4 1.7 %collective-permute-done.part1 = bf16[256,512]{1,0:T(8,128)(2,1)S(1)} collective-permute-done((bf16[256,512]{1,0:T(8,128)(2,1)S(1)}, bf16[256,512]{1,0:T(8,128)(2,1)S(1)}, u32[]{:S(2)}, u32[]{:S(2)}) %collective-permute-start) | collective-permute-done | bytes 262176 | tf_op jit(solution)/shard_map/ppermute | solution.py:15
  47.1 11.2 %collective-permute-done.2.part3 = bf16[256,512]{1,0:T(8,128)(2,1)S(1)} collective-permute-done((bf16[256,512]{1,0:T(8,128)(2,1)S(1)}, bf16[256,512]{1,0:T(8,128)(2,1)S(1)}, u32[]{:S(2)}, u32[]{:S(2)}) %collective-permute-start.2) | collective-permute-done | bytes 262176 | tf_op jit(solution)/shard_map/ppermute | solution.py:15
  58.3 1.4 %shard_map.83 = (bf16[1024,512]{1,0:T(8,128)(2,1)S(1)}, bf16[256,512]{1,0:T(8,128)(2,1)S(1)}, bf16[256,512]{1,0:T(8,128)(2,1)S(1)}) custom-call(s32[3,2,4]{2,1,0:T(2,128)S(1)} %get-tuple-element.21.off_rows, s32[3,2,4]{2,1,0:T(2,128)S(1)} %get-tuple-element.22.off_mask, bf16[3,2,4,128,128]{4,3,2,1,0:T(8,128)(2,1)S(1)} %get-tuple-element.23.off_tiles, ...), custom_call_target="tpu_custom_call" | custom-call | tf_op jit(solution)/shard_map/pallas_call | solution.py:150
  59.7 1.1 %shard_map.87 = bf16[256,512]{1,0:T(8,128)(2,1)S(1)} custom-call(s32[3,2,4]{2,1,0:T(2,128)S(1)} %get-tuple-element.21.off_rows, s32[3,2,4]{2,1,0:T(2,128)S(1)} %get-tuple-element.22.off_mask, bf16[3,2,4,128,128]{4,3,2,1,0:T(8,128)(2,1)S(1)} %get-tuple-element.23.off_tiles, bf16[1024,512]{1,0:T(8,128)(2,1)S(1)} %get-tuple-element.25.gathered), custom_call_target="tpu_custom_call" | custom-call | tf_op jit(solution)/shard_map/pallas_call | solution.py:150
  60.8 5.1 %collective-permute-start.7 = (bf16[256,512]{1,0:T(8,128)(2,1)S(1)}, bf16[256,512]{1,0:T(8,128)(2,1)S(1)}, u32[]{:S(2)}, u32[]{:S(2)}) collective-permute-start(bf16[256,512]{1,0:T(8,128)(2,1)S(1)} %shard_map.87), channel_id=1, source_target_pairs={{0,4},{4,0},{8,12},{12,8},{16,20},{20,16},{24,28},{28,24},{32,36},... | collective-permute-start | bytes 786440 | tf_op jit(solution)/shard_map/ppermute | solution.py:15
  65.9 5.2 %collective-permute-start.11 = (bf16[256,512]{1,0:T(8,128)(2,1)S(1)}, bf16[256,512]{1,0:T(8,128)(2,1)S(1)}, u32[]{:S(2)}, u32[]{:S(2)}) collective-permute-start(bf16[256,512]{1,0:T(8,128)(2,1)S(1)} %get-tuple-element.30), channel_id=1, source_target_pairs={{0,256},{4,260},{8,264},{12,268},{16,272},{20,276},{24,280},{28,28... | collective-permute-start | bytes 786440 | tf_op jit(solution)/shard_map/ppermute | solution.py:15
  71.1 2.1 %collective-permute-start.8 = (bf16[256,512]{1,0:T(8,128)(2,1)S(1)}, bf16[256,512]{1,0:T(8,128)(2,1)S(1)}, u32[]{:S(2)}, u32[]{:S(2)}) collective-permute-start(bf16[256,512]{1,0:T(8,128)(2,1)S(1)} %get-tuple-element.28), channel_id=1, source_target_pairs={{0,32},{4,36},{8,40},{12,44},{16,48},{20,52},{24,56},{28,60},{32,0... | collective-permute-start | bytes 786440 | tf_op jit(solution)/shard_map/ppermute | solution.py:15
  73.2 0.0 collective-permute-done.6.got1
  73.2 1.0 %shard_map.86 = f32[256,512]{1,0:T(8,128)S(1)} custom-call(s32[2,4]{1,0:T(2,128)S(1)} %get-tuple-element.18.diag_cols, s32[2,4]{1,0:T(2,128)S(1)} %get-tuple-element.19.diag_mask, bf16[2,4,128,128]{3,2,1,0:T(8,128)(2,1)S(1)} %get-tuple-element.20.diag_tiles, bf16[1024,512]{1,0:T(8,128)(2,1)S(1)} %get-tuple-element.25.gathered, ...), custom_call_target="tpu_custom_call" | custom-call | tf_op jit(solution)/shard_map/pallas_call | solution.py:150
  74.3 10.9 %collective-permute-done.11 = bf16[256,512]{1,0:T(8,128)(2,1)S(1)} collective-permute-done((bf16[256,512]{1,0:T(8,128)(2,1)S(1)}, bf16[256,512]{1,0:T(8,128)(2,1)S(1)}, u32[]{:S(2)}, u32[]{:S(2)}) %collective-permute-start.11) | collective-permute-done | bytes 262176 | tf_op jit(solution)/shard_map/ppermute | solution.py:15
  85.2 0.0 collective-permute-done.8
  85.2 1.0 %convert_add_fusion = f32[256,512]{1,0:T(8,128)} fusion(bf16[256,512]{1,0:T(8,128)(2,1)S(1)} %collective-permute-done.11, bf16[256,512]{1,0:T(8,128)(2,1)S(1)} %collective-permute-done.10, bf16[256,512]{1,0:T(8,128)(2,1)S(1)} %collective-permute-done.8, f32[256,512]{1,0:T(8,128)S(1)} %shard_map.86, bf16[256,512]{1,0:T(8,128)(2,1)S(1)} %collective-permute-done.7), kind=kLoop, calls=%fused_computation | loop fusion | flops 1048576 | bytes 2097152 | tf_op jit(solution)/shard_map/add | solution.py:213
  (4 shorter events, 0.0 us)
Async XLA Ops:
  1.6 21.4 %collective-permute-start.4 = (bf16[256,512]{1,0:T(8,128)(2,1)S(1)}, bf16[256,512]{1,0:T(8,128)(2,1)S(1)}, u32[]{:S(2)}, u32[]{:S(2)}) collective-permute-start(bf16[256,512]{1,0:T(8,128)(2,1)S(1)} %get-tuple-element.24.part0.own), channel_id=1, source_target_pairs={{0,4},{4,0},{8,12},{12,8},{16,20},{20,16},{24,28},{28,24},{32,36},... | collective-permute-start | bytes 786440 | tf_op jit(solution)/shard_map/ppermute | solution.py:15
  10.3 12.6 %collective-permute-start.5 = (bf16[256,512]{1,0:T(8,128)(2,1)S(1)}, bf16[256,512]{1,0:T(8,128)(2,1)S(1)}, u32[]{:S(2)}, u32[]{:S(2)}) collective-permute-start(bf16[256,512]{1,0:T(8,128)(2,1)S(1)} %get-tuple-element.24.part0.own), channel_id=1, source_target_pairs={{0,32},{4,36},{8,40},{12,44},{16,48},{20,52},{24,56},{28,60},{32,0... | collective-permute-start | bytes 786440 | tf_op jit(solution)/shard_map/ppermute | solution.py:15
  12.3 19.3 %collective-permute-start.3 = (bf16[256,512]{1,0:T(8,128)(2,1)S(1)}, bf16[256,512]{1,0:T(8,128)(2,1)S(1)}, u32[]{:S(2)}, u32[]{:S(2)}) collective-permute-start(bf16[256,512]{1,0:T(8,128)(2,1)S(1)} %get-tuple-element.24.part0.own), channel_id=1, source_target_pairs={{0,256},{4,260},{8,264},{12,268},{16,272},{20,276},{24,280},{28,28... | collective-permute-start | bytes 786440 | tf_op jit(solution)/shard_map/ppermute | solution.py:15
  17.1 20.8 %collective-permute-start.1 = (bf16[256,512]{1,0:T(8,128)(2,1)S(1)}, bf16[256,512]{1,0:T(8,128)(2,1)S(1)}, u32[]{:S(2)}, u32[]{:S(2)}) collective-permute-start(bf16[256,512]{1,0:T(8,128)(2,1)S(1)} %get-tuple-element.24.part0.own), channel_id=1, source_target_pairs={{0,2},{1,3},{2,0},{3,1},{4,6},{5,7},{6,4},{7,5},{8,10},{9,11},{10,... | collective-permute-start | bytes 786440 | tf_op jit(solution)/shard_map/ppermute | solution.py:15
  32.6 10.6 %collective-permute-start.9 = (bf16[256,512]{1,0:T(8,128)(2,1)S(1)}, bf16[256,512]{1,0:T(8,128)(2,1)S(1)}, u32[]{:S(2)}, u32[]{:S(2)}) collective-permute-start(bf16[256,512]{1,0:T(8,128)(2,1)S(1)} %get-tuple-element.29), channel_id=1, source_target_pairs={{0,1},{1,0},{2,3},{3,2},{4,5},{5,4},{6,7},{7,6},{8,9},{9,8},{10,11... | collective-permute-start | bytes 786440 | tf_op jit(solution)/shard_map/ppermute | solution.py:15
  34.6 12.5 %collective-permute-start = (bf16[256,512]{1,0:T(8,128)(2,1)S(1)}, bf16[256,512]{1,0:T(8,128)(2,1)S(1)}, u32[]{:S(2)}, u32[]{:S(2)}) collective-permute-start(bf16[256,512]{1,0:T(8,128)(2,1)S(1)} %get-tuple-element.24.part0.own), channel_id=1, source_target_pairs={{0,1},{1,0},{2,3},{3,2},{4,5},{5,4},{6,7},{7,6},{8,9},{9,8},{10,11... | collective-permute-start | bytes 786440 | tf_op jit(solution)/shard_map/ppermute | solution.py:15
  37.9 20.4 %collective-permute-start.2 = (bf16[256,512]{1,0:T(8,128)(2,1)S(1)}, bf16[256,512]{1,0:T(8,128)(2,1)S(1)}, u32[]{:S(2)}, u32[]{:S(2)}) collective-permute-start(bf16[256,512]{1,0:T(8,128)(2,1)S(1)} %collective-permute-done.1.part2), channel_id=1, source_target_pairs={{0,1},{1,0},{2,3},{3,2},{4,5},{5,4},{6,7},{7,6},{8,9},{9,8},{10,11... | collective-permute-start | bytes 786440 | tf_op jit(solution)/shard_map/ppermute | solution.py:15
  39.9 33.4 %collective-permute-start.6 = (bf16[256,512]{1,0:T(8,128)(2,1)S(1)}, bf16[256,512]{1,0:T(8,128)(2,1)S(1)}, u32[]{:S(2)}, u32[]{:S(2)}) collective-permute-start(bf16[256,512]{1,0:T(8,128)(2,1)S(1)} %get-tuple-element.27), channel_id=1, source_target_pairs={{0,1},{1,0},{2,3},{3,2},{4,5},{5,4},{6,7},{7,6},{8,9},{9,8},{10,11... | collective-permute-start | bytes 786440 | tf_op jit(solution)/shard_map/ppermute | solution.py:15
  43.3 29.9 %copy-start = (f32[256,512]{1,0:T(8,128)S(1)}, f32[256,512]{1,0:T(8,128)}, u32[]{:S(2)}) copy-start(f32[256,512]{1,0:T(8,128)} %vectors.3) | copy-start | bytes 1572868
  43.3 29.9 %copy-start.1 = (f32[256,512]{1,0:T(8,128)S(1)}, f32[256,512]{1,0:T(8,128)}, u32[]{:S(2)}) copy-start(f32[256,512]{1,0:T(8,128)} %previous.1) | copy-start | bytes 1572868
  43.4 30.9 %collective-permute-start.10 = (bf16[256,512]{1,0:T(8,128)(2,1)S(1)}, bf16[256,512]{1,0:T(8,128)(2,1)S(1)}, u32[]{:S(2)}, u32[]{:S(2)}) collective-permute-start(bf16[256,512]{1,0:T(8,128)(2,1)S(1)} %add_convert_fusion), channel_id=1, source_target_pairs={{0,2},{1,3},{2,0},{3,1},{4,6},{5,7},{6,4},{7,5},{8,10},{9,11},{10,... | collective-permute-start | bytes 786440 | tf_op jit(solution)/shard_map/ppermute | solution.py:15
  60.8 13.5 %collective-permute-start.7 = (bf16[256,512]{1,0:T(8,128)(2,1)S(1)}, bf16[256,512]{1,0:T(8,128)(2,1)S(1)}, u32[]{:S(2)}, u32[]{:S(2)}) collective-permute-start(bf16[256,512]{1,0:T(8,128)(2,1)S(1)} %shard_map.87), channel_id=1, source_target_pairs={{0,4},{4,0},{8,12},{12,8},{16,20},{20,16},{24,28},{28,24},{32,36},... | collective-permute-start | bytes 786440 | tf_op jit(solution)/shard_map/ppermute | solution.py:15
  65.9 19.3 %collective-permute-start.11 = (bf16[256,512]{1,0:T(8,128)(2,1)S(1)}, bf16[256,512]{1,0:T(8,128)(2,1)S(1)}, u32[]{:S(2)}, u32[]{:S(2)}) collective-permute-start(bf16[256,512]{1,0:T(8,128)(2,1)S(1)} %get-tuple-element.30), channel_id=1, source_target_pairs={{0,256},{4,260},{8,264},{12,268},{16,272},{20,276},{24,280},{28,28... | collective-permute-start | bytes 786440 | tf_op jit(solution)/shard_map/ppermute | solution.py:15
  71.1 14.1 %collective-permute-start.8 = (bf16[256,512]{1,0:T(8,128)(2,1)S(1)}, bf16[256,512]{1,0:T(8,128)(2,1)S(1)}, u32[]{:S(2)}, u32[]{:S(2)}) collective-permute-start(bf16[256,512]{1,0:T(8,128)(2,1)S(1)} %get-tuple-element.28), channel_id=1, source_target_pairs={{0,32},{4,36},{8,40},{12,44},{16,48},{20,52},{24,56},{28,60},{32,0... | collective-permute-start | bytes 786440 | tf_op jit(solution)/shard_map/ppermute | solution.py:15

commit v2 on v1

--- a/solution.py
+++ b/solution.py
@@ -69,7 +69,9 @@
             )
 
 
-def early_kernel(diag_cols, diag_mask, off_rows, off_mask, diag_tiles, off_tiles, own, arr0, arr1, acc):
+def scatter_kernel(
+    diag_cols, diag_mask, off_rows, off_mask, diag_tiles, off_tiles, own, arr0, arr1, arr2, acc, out1, out3,
+):
     strips, _, size, _ = diag_tiles.shape
     shift = strips * lax.axis_index("qtr")
     acc[...] = jnp.zeros_like(acc)
@@ -78,46 +80,31 @@
             acc, diag_tiles.at[strip], lambda i: diag_mask[strip, i], lambda i: diag_cols[strip, i],
             True, own[strip * size:(strip + 1) * size, :], shift,
         )
-    partner_spread(acc, (0, 1), (arr0, arr1), off_rows, off_mask, off_tiles, shift)
-
-
-def late_kernel(off_rows, off_mask, off_tiles, arr2, before, acc, out1, out3):
-    strips, _, size, _ = off_tiles.shape[1:]
-    shift = strips * lax.axis_index("qtr")
-    partner_spread(acc, (2,), (arr2,), off_rows, off_mask, off_tiles, shift)
+    partner_spread(acc, (0, 1, 2), (arr0, arr1, arr2), off_rows, off_mask, off_tiles, shift)
     span = strips * size
     out1[...] = acc[span:2 * span, :].astype(jnp.bfloat16)
     out3[...] = acc[3 * span:, :].astype(jnp.bfloat16)
 
 
-def collect(parts, gathered):
-    span = parts[0].shape[0]
-    for i, part in enumerate(parts):
-        gathered[i * span:(i + 1) * span, :] = part[...]
-
-
 def partner_products(partner, out, off_rows, off_mask, off_tiles, gathered, shift):
     strips, slots, size, _ = off_tiles.shape[1:]
     for strip in range(strips):
-        total = None
+        tiles, blocks = [], []
         for slot in range(slots):
             place = pl.multiple_of((off_rows[partner, strip, slot] ^ shift) * size, size)
-            tile = live(off_tiles[partner, strip, slot], off_mask[partner, strip, slot])
-            term = dot_flipped(tile, gathered[pl.ds(place, size), :])
-            total = term if total is None else total + term
+            tiles.append(live(off_tiles[partner, strip, slot], off_mask[partner, strip, slot]))
+            blocks.append(gathered[pl.ds(place, size), :])
+        total = dot_flipped(jnp.concatenate(tiles, 0), jnp.concatenate(blocks, 0))
         out[strip * size:(strip + 1) * size, :] = total.astype(out.dtype)
 
 
-def outer_kernel(off_rows, off_mask, off_tiles, part0, part1, part2, part3, gathered, out2, out1):
+def partner_kernel(off_rows, off_mask, off_tiles, part0, part1, part2, part3, gathered, out2, out1, out0):
+    span = part0.shape[0]
     shift = off_tiles.shape[1] * lax.axis_index("qtr")
-    collect((part0, part1, part2, part3), gathered)
-    partner_products(2, out2, off_rows, off_mask, off_tiles, gathered, shift)
-    partner_products(1, out1, off_rows, off_mask, off_tiles, gathered, shift)
-
-
-def inner_kernel(off_rows, off_mask, off_tiles, gathered, out0):
-    shift = off_tiles.shape[1] * lax.axis_index("qtr")
-    partner_products(0, out0, off_rows, off_mask, off_tiles, gathered, shift)
+    for i, part in enumerate((part0, part1, part2, part3)):
+        gathered[i * span:(i + 1) * span, :] = part[...]
+    for partner, out in ((2, out2), (1, out1), (0, out0)):
+        partner_products(partner, out, off_rows, off_mask, off_tiles, gathered, shift)
 
 
 def base_kernel(diag_cols, diag_mask, diag_tiles, gathered, acc, got1, vectors, previous, base):
@@ -168,8 +155,8 @@
     group_half = ((quarters * rows, width), jnp.bfloat16)
     group_full = ((quarters * rows, width), jnp.float32)
 
-    stored = (diag_tiles, off_tiles, diag_cols, diag_mask, off_rows, off_mask)
-    own, diag_tiles, off_tiles, diag_cols, diag_mask, off_rows, off_mask = call(
+    stored = (diag_tiles, diag_cols, diag_mask, off_rows, off_mask)
+    own, diag_tiles, diag_cols, diag_mask, off_rows, off_mask = call(
         load_kernel, (), (), (half, *[(x.shape, x.dtype) for x in stored]),
         [pltpu.VMEM((rows, width), jnp.float32), pltpu.SemaphoreType.DMA((4 + len(stored),))],
         (vectors, *stored),
@@ -181,13 +168,9 @@
     arr0 = swap(own, "grp", bits[0])
     part3 = swap(part2, "qtr", 1)
 
-    (acc,) = call(
-        early_kernel, (diag_cols, diag_mask, off_rows, off_mask),
-        (diag_tiles, off_tiles, own, arr0, arr1), (group_full,), [],
-    )
     acc, send1, send3 = call(
-        late_kernel, (off_rows, off_mask), (off_tiles, arr2, acc),
-        (group_full, half, half), [], aliases={4: 0},
+        scatter_kernel, (diag_cols, diag_mask, off_rows, off_mask),
+        (diag_tiles, off_tiles, own, arr0, arr1, arr2), (group_full, half, half), [],
     )
     got3 = swap(send3, "qtr", 1)
     send2 = (acc[2 * rows:3 * rows] + got3.astype(jnp.float32)).astype(jnp.bfloat16)
@@ -195,13 +178,12 @@
     got1 = swap(send1, "qtr", 1)
 
     parts = (own, part1, part2, part3)
-    gathered, away2, away1 = call(
-        outer_kernel, (off_rows, off_mask), (off_tiles, *parts),
-        (group_half, half, half), [],
+    gathered, away2, away1, away0 = call(
+        partner_kernel, (off_rows, off_mask), (off_tiles, *parts),
+        (group_half, half, half, half), [],
     )
     back2 = swap(away2, "grp", bits[2])
     back1 = swap(away1, "grp", bits[1])
-    (away0,) = call(inner_kernel, (off_rows, off_mask), (off_tiles, gathered), (half,), [])
     back0 = swap(away0, "grp", bits[0])
     (base,) = call(
         base_kernel, (diag_cols, diag_mask),

time: 86.6 us -> 70.3 us (0.81)
  waiting for transfers between devices: 30.6 us -> 14.4 us
  Pallas kernels: 7.98 us -> 5.82 us
  local copies, waits for them, and re-layouts: 0.01 us -> 1.14 us
  starting transfers between devices: 46.3 us -> 47.2 us
    ppermute x12, waiting for transfers between devices: 30.6 us -> 14.4 us  [swap(): return lax.ppermute(block, axis, [(i, i ^ mask) for i in range(count)])]
    pallas_call x6 -> x4, Pallas kernels: 7.98 us -> 5.82 us  [call(): pl.pallas_call(kernel, in_specs=[smem] * len(scalars) + [vmem] * len(arra...]
    unnamed x4 -> x8, local copies, waits for them, and re-layouts: 0.01 us -> 1.14 us
    ppermute x12, starting transfers between devices: 46.3 us -> 47.2 us  [swap(): return lax.ppermute(block, axis, [(i, i ^ mask) for i in range(count)])]
  transfers between devices with their start and end apart: 12 -> 12, of which waited for: 4 -> 3; matrix products, arithmetic and copies ran while one was open for 0% -> 0% of each run, Pallas kernels for 7% -> 6%
where the time goes in v2:
time: 70.3 us; the launch traced here: 69.8 us
  starting transfers between devices  47.2 us (67%)
  waiting for transfers between devices  14.4 us (20%)
  Pallas kernels  5.82 us (8%)
  local copies, waits for them, and re-layouts  1.14 us (2%)
  other arithmetic  1.04 us (1%)
    ppermute x12, starting transfers between devices, swap(): return lax.ppermute(block, axis, [(i, i ^ mask) for i in range(count)])  47.2 us
    ppermute x12, waiting for transfers between devices, swap(): return lax.ppermute(block, axis, [(i, i ^ mask) for i in range(count)])  14.4 us
    pallas_call x4, Pallas kernels, call(): pl.pallas_call(kernel, in_specs=[smem] * len(scalars) + [vmem] * len(arra...  5.82 us
  transfers between devices with their start and end apart: 12, of which 3 were waited for; matrix products, arithmetic and copies ran while one was open for 0% of the time, Pallas kernels for 6%

profile of v2, /device:TPU:1, one launch (start us, length us, event | category | flops | bytes accessed | tf_op | source)
XLA Modules:
  0.0 69.8 jit_solution(1785920383564785520)
XLA Ops:
  0.0 1.4 %shard_map.82 = (bf16[256,512]{1,0:T(8,128)(2,1)S(1)}, bf16[2,4,128,128]{3,2,1,0:T(8,128)(2,1)S(1)}, s32[2,4]{1,0:T(2,128)S(1)}, s32[2,4]{1,0:T(2,128)S(1)}, s32...) custom-call(f32[256,512]{1,0:T(8,128)} %vectors.3, bf16[2,4,128,128]{3,2,1,0:T(8,128)(2,1)} %refs_0_.1, s32[2,4]{1,0:T(2,128)} %refs_1_.1, ...), custom_call_target="tpu_custom_call" | custom-call | tf_op jit(solution)/shard_map/pallas_call | solution.py:137
  1.4 6.6 %collective-permute-start.1 = (bf16[256,512]{1,0:T(8,128)(2,1)S(1)}, bf16[256,512]{1,0:T(8,128)(2,1)S(1)}, u32[]{:S(2)}, u32[]{:S(2)}) collective-permute-start(bf16[256,512]{1,0:T(8,128)(2,1)S(1)} %get-tuple-element.23.part0.own), channel_id=1, source_target_pairs={{0,2},{1,3},{2,0},{3,1},{4,6},{5,7},{6,4},{7,5},{8,10},{9,11},{10,... | collective-permute-start | bytes 786440 | tf_op jit(solution)/shard_map/ppermute | solution.py:15
  8.0 7.5 %collective-permute-start.5 = (bf16[256,512]{1,0:T(8,128)(2,1)S(1)}, bf16[256,512]{1,0:T(8,128)(2,1)S(1)}, u32[]{:S(2)}, u32[]{:S(2)}) collective-permute-start(bf16[256,512]{1,0:T(8,128)(2,1)S(1)} %get-tuple-element.23.part0.own), channel_id=1, source_target_pairs={{0,256},{4,260},{8,264},{12,268},{16,272},{20,276},{24,280},{28,28... | collective-permute-start | bytes 786440 | tf_op jit(solution)/shard_map/ppermute | solution.py:15
  15.5 4.7 %collective-permute-start.4 = (bf16[256,512]{1,0:T(8,128)(2,1)S(1)}, bf16[256,512]{1,0:T(8,128)(2,1)S(1)}, u32[]{:S(2)}, u32[]{:S(2)}) collective-permute-start(bf16[256,512]{1,0:T(8,128)(2,1)S(1)} %get-tuple-element.23.part0.own), channel_id=1, source_target_pairs={{0,32},{4,36},{8,40},{12,44},{16,48},{20,52},{24,56},{28,60},{32,0... | collective-permute-start | bytes 786440 | tf_op jit(solution)/shard_map/ppermute | solution.py:15
  20.1 3.4 %collective-permute-start.3 = (bf16[256,512]{1,0:T(8,128)(2,1)S(1)}, bf16[256,512]{1,0:T(8,128)(2,1)S(1)}, u32[]{:S(2)}, u32[]{:S(2)}) collective-permute-start(bf16[256,512]{1,0:T(8,128)(2,1)S(1)} %get-tuple-element.23.part0.own), channel_id=1, source_target_pairs={{0,4},{4,0},{8,12},{12,8},{16,20},{20,16},{24,28},{28,24},{32,36},... | collective-permute-start | bytes 786440 | tf_op jit(solution)/shard_map/ppermute | solution.py:15
  23.6 4.0 %collective-permute-start = (bf16[256,512]{1,0:T(8,128)(2,1)S(1)}, bf16[256,512]{1,0:T(8,128)(2,1)S(1)}, u32[]{:S(2)}, u32[]{:S(2)}) collective-permute-start(bf16[256,512]{1,0:T(8,128)(2,1)S(1)} %get-tuple-element.23.part0.own), channel_id=1, source_target_pairs={{0,1},{1,0},{2,3},{3,2},{4,5},{5,4},{6,7},{7,6},{8,9},{9,8},{10,11... | collective-permute-start | bytes 786440 | tf_op jit(solution)/shard_map/ppermute | solution.py:15
  27.6 0.0 collective-permute-done.1.part2
  27.6 1.9 %collective-permute-start.2 = (bf16[256,512]{1,0:T(8,128)(2,1)S(1)}, bf16[256,512]{1,0:T(8,128)(2,1)S(1)}, u32[]{:S(2)}, u32[]{:S(2)}) collective-permute-start(bf16[256,512]{1,0:T(8,128)(2,1)S(1)} %collective-permute-done.1.part2), channel_id=1, source_target_pairs={{0,1},{1,0},{2,3},{3,2},{4,5},{5,4},{6,7},{7,6},{8,9},{9,8},{10,11... | collective-permute-start | bytes 786440 | tf_op jit(solution)/shard_map/ppermute | solution.py:15
  29.5 0.0 collective-permute-done.5.arr2
  29.5 0.0 collective-permute-done.4.arr1
  29.5 0.0 collective-permute-done.3.arr0
  29.5 0.0 copy-start
  29.5 1.1 %copy-done = bf16[3,2,4,128,128]{4,3,2,1,0:T(8,128)(2,1)S(1)} copy-done((bf16[3,2,4,128,128]{4,3,2,1,0:T(8,128)(2,1)S(1)}, bf16[3,2,4,128,128]{4,3,2,1,0:T(8,128)(2,1)}, u32[]{:S(2)}) %copy-start) | copy-done | bytes 786456
  30.7 2.2 %shard_map.84 = (f32[1024,512]{1,0:T(8,128)S(1)}, bf16[256,512]{1,0:T(8,128)(2,1)S(1)}, bf16[256,512]{1,0:T(8,128)(2,1)S(1)}) custom-call(s32[2,4]{1,0:T(2,128)S(1)} %get-tuple-element.18.diag_cols, s32[2,4]{1,0:T(2,128)S(1)} %get-tuple-element.19.diag_mask, s32[3,2,4]{2,1,0:T(2,128)S(1)} %get-tuple-element.21.off_rows, ...), custom_call_target="tpu_custom_call" | custom-call | tf_op jit(solution)/shard_map/pallas_call | solution.py:137
  32.8 3.4 %collective-permute-start.9 = (bf16[256,512]{1,0:T(8,128)(2,1)S(1)}, bf16[256,512]{1,0:T(8,128)(2,1)S(1)}, u32[]{:S(2)}, u32[]{:S(2)}) collective-permute-start(bf16[256,512]{1,0:T(8,128)(2,1)S(1)} %get-tuple-element.29), channel_id=1, source_target_pairs={{0,1},{1,0},{2,3},{3,2},{4,5},{5,4},{6,7},{7,6},{8,9},{9,8},{10,11... | collective-permute-start | bytes 786440 | tf_op jit(solution)/shard_map/ppermute | solution.py:15
  36.2 1.9 %collective-permute-start.6 = (bf16[256,512]{1,0:T(8,128)(2,1)S(1)}, bf16[256,512]{1,0:T(8,128)(2,1)S(1)}, u32[]{:S(2)}, u32[]{:S(2)}) collective-permute-start(bf16[256,512]{1,0:T(8,128)(2,1)S(1)} %get-tuple-element.26), channel_id=1, source_target_pairs={{0,1},{1,0},{2,3},{3,2},{4,5},{5,4},{6,7},{7,6},{8,9},{9,8},{10,11... | collective-permute-start | bytes 786440 | tf_op jit(solution)/shard_map/ppermute | solution.py:15
  38.1 0.0 collective-permute-done.part1
  38.1 1.7 %collective-permute-done.2.part3 = bf16[256,512]{1,0:T(8,128)(2,1)S(1)} collective-permute-done((bf16[256,512]{1,0:T(8,128)(2,1)S(1)}, bf16[256,512]{1,0:T(8,128)(2,1)S(1)}, u32[]{:S(2)}, u32[]{:S(2)}) %collective-permute-start.2) | collective-permute-done | bytes 262176 | tf_op jit(solution)/shard_map/ppermute | solution.py:15
  39.8 1.3 %shard_map.83 = (bf16[1024,512]{1,0:T(8,128)(2,1)S(1)}, bf16[256,512]{1,0:T(8,128)(2,1)S(1)}, bf16[256,512]{1,0:T(8,128)(2,1)S(1)}, bf16[256,512]{1,0:T(8,128)(2,1)S(1)}) custom-call(s32[3,2,4]{2,1,0:T(2,128)S(1)} %get-tuple-element.21.off_rows, s32[3,2,4]{2,1,0:T(2,128)S(1)} %get-tuple-element.22.off_mask, bf16[3,2,4,128,128]{4,3,2,1,0:T(8,128)(2,1)S(1)} %copy-done.1, ...), custom_call_target="tpu_custom_call" | custom-call | tf_op jit(solution)/shard_map/pallas_call | solution.py:137
  41.1 2.7 %collective-permute-start.7 = (bf16[256,512]{1,0:T(8,128)(2,1)S(1)}, bf16[256,512]{1,0:T(8,128)(2,1)S(1)}, u32[]{:S(2)}, u32[]{:S(2)}) collective-permute-start(bf16[256,512]{1,0:T(8,128)(2,1)S(1)} %get-tuple-element.27), channel_id=1, source_target_pairs={{0,4},{4,0},{8,12},{12,8},{16,20},{20,16},{24,28},{28,24},{32,36},... | collective-permute-start | bytes 786440 | tf_op jit(solution)/shard_map/ppermute | solution.py:15
  43.8 2.1 %collective-permute-start.8 = (bf16[256,512]{1,0:T(8,128)(2,1)S(1)}, bf16[256,512]{1,0:T(8,128)(2,1)S(1)}, u32[]{:S(2)}, u32[]{:S(2)}) collective-permute-start(bf16[256,512]{1,0:T(8,128)(2,1)S(1)} %get-tuple-element.28), channel_id=1, source_target_pairs={{0,32},{4,36},{8,40},{12,44},{16,48},{20,52},{24,56},{28,60},{32,0... | collective-permute-start | bytes 786440 | tf_op jit(solution)/shard_map/ppermute | solution.py:15
  46.0 7.1 %collective-permute-start.11 = (bf16[256,512]{1,0:T(8,128)(2,1)S(1)}, bf16[256,512]{1,0:T(8,128)(2,1)S(1)}, u32[]{:S(2)}, u32[]{:S(2)}) collective-permute-start(bf16[256,512]{1,0:T(8,128)(2,1)S(1)} %get-tuple-element.30), channel_id=1, source_target_pairs={{0,256},{4,260},{8,264},{12,268},{16,272},{20,276},{24,280},{28,28... | collective-permute-start | bytes 786440 | tf_op jit(solution)/shard_map/ppermute | solution.py:15
  53.1 0.0 collective-permute-done.9
  53.1 0.1 add_convert_fusion
  53.2 1.9 %collective-permute-start.10 = (bf16[256,512]{1,0:T(8,128)(2,1)S(1)}, bf16[256,512]{1,0:T(8,128)(2,1)S(1)}, u32[]{:S(2)}, u32[]{:S(2)}) collective-permute-start(bf16[256,512]{1,0:T(8,128)(2,1)S(1)} %add_convert_fusion), channel_id=1, source_target_pairs={{0,2},{1,3},{2,0},{3,1},{4,6},{5,7},{6,4},{7,5},{8,10},{9,11},{10,... | collective-permute-start | bytes 786440 | tf_op jit(solution)/shard_map/ppermute | solution.py:15
  55.1 0.0 collective-permute-done.6.got1
  55.1 1.0 %shard_map.85 = f32[256,512]{1,0:T(8,128)S(1)} custom-call(s32[2,4]{1,0:T(2,128)S(1)} %get-tuple-element.18.diag_cols, s32[2,4]{1,0:T(2,128)S(1)} %get-tuple-element.19.diag_mask, bf16[2,4,128,128]{3,2,1,0:T(8,128)(2,1)S(1)} %get-tuple-element.20.diag_tiles, bf16[1024,512]{1,0:T(8,128)(2,1)S(1)} %get-tuple-element.24.gathered, ...), custom_call_target="tpu_custom_call" | custom-call | tf_op jit(solution)/shard_map/pallas_call | solution.py:137
  56.2 0.0 collective-permute-done.7
  56.2 0.0 collective-permute-done.8
  56.2 5.0 %collective-permute-done.11 = bf16[256,512]{1,0:T(8,128)(2,1)S(1)} collective-permute-done((bf16[256,512]{1,0:T(8,128)(2,1)S(1)}, bf16[256,512]{1,0:T(8,128)(2,1)S(1)}, u32[]{:S(2)}, u32[]{:S(2)}) %collective-permute-start.11) | collective-permute-done | bytes 262176 | tf_op jit(solution)/shard_map/ppermute | solution.py:15
  61.2 7.6 %collective-permute-done.10 = bf16[256,512]{1,0:T(8,128)(2,1)S(1)} collective-permute-done((bf16[256,512]{1,0:T(8,128)(2,1)S(1)}, bf16[256,512]{1,0:T(8,128)(2,1)S(1)}, u32[]{:S(2)}, u32[]{:S(2)}) %collective-permute-start.10) | collective-permute-done | bytes 262176 | tf_op jit(solution)/shard_map/ppermute | solution.py:15
  68.9 1.0 %convert_add_fusion = f32[256,512]{1,0:T(8,128)} fusion(bf16[256,512]{1,0:T(8,128)(2,1)S(1)} %collective-permute-done.11, bf16[256,512]{1,0:T(8,128)(2,1)S(1)} %collective-permute-done.10, bf16[256,512]{1,0:T(8,128)(2,1)S(1)} %collective-permute-done.8, f32[256,512]{1,0:T(8,128)S(1)} %shard_map.85, bf16[256,512]{1,0:T(8,128)(2,1)S(1)} %collective-permute-done.7), kind=kLoop, calls=%fused_computation | loop fusion | flops 1048576 | bytes 2097152 | tf_op jit(solution)/shard_map/add | solution.py:195
  (6 shorter events, 0.0 us)
Async XLA Ops:
  0.0 39.8 %copy-start.1 = (bf16[3,2,4,128,128]{4,3,2,1,0:T(8,128)(2,1)S(1)}, bf16[3,2,4,128,128]{4,3,2,1,0:T(8,128)(2,1)}, u32[]{:S(2)}) copy-start(bf16[3,2,4,128,128]{4,3,2,1,0:T(8,128)(2,1)} %off_tiles.3) | copy-start | bytes 2359300
  1.4 26.2 %collective-permute-start.1 = (bf16[256,512]{1,0:T(8,128)(2,1)S(1)}, bf16[256,512]{1,0:T(8,128)(2,1)S(1)}, u32[]{:S(2)}, u32[]{:S(2)}) collective-permute-start(bf16[256,512]{1,0:T(8,128)(2,1)S(1)} %get-tuple-element.23.part0.own), channel_id=1, source_target_pairs={{0,2},{1,3},{2,0},{3,1},{4,6},{5,7},{6,4},{7,5},{8,10},{9,11},{10,... | collective-permute-start | bytes 786440 | tf_op jit(solution)/shard_map/ppermute | solution.py:15
  8.0 21.5 %collective-permute-start.5 = (bf16[256,512]{1,0:T(8,128)(2,1)S(1)}, bf16[256,512]{1,0:T(8,128)(2,1)S(1)}, u32[]{:S(2)}, u32[]{:S(2)}) collective-permute-start(bf16[256,512]{1,0:T(8,128)(2,1)S(1)} %get-tuple-element.23.part0.own), channel_id=1, source_target_pairs={{0,256},{4,260},{8,264},{12,268},{16,272},{20,276},{24,280},{28,28... | collective-permute-start | bytes 786440 | tf_op jit(solution)/shard_map/ppermute | solution.py:15
  15.5 14.1 %collective-permute-start.4 = (bf16[256,512]{1,0:T(8,128)(2,1)S(1)}, bf16[256,512]{1,0:T(8,128)(2,1)S(1)}, u32[]{:S(2)}, u32[]{:S(2)}) collective-permute-start(bf16[256,512]{1,0:T(8,128)(2,1)S(1)} %get-tuple-element.23.part0.own), channel_id=1, source_target_pairs={{0,32},{4,36},{8,40},{12,44},{16,48},{20,52},{24,56},{28,60},{32,0... | collective-permute-start | bytes 786440 | tf_op jit(solution)/shard_map/ppermute | solution.py:15
  20.1 9.4 %collective-permute-start.3 = (bf16[256,512]{1,0:T(8,128)(2,1)S(1)}, bf16[256,512]{1,0:T(8,128)(2,1)S(1)}, u32[]{:S(2)}, u32[]{:S(2)}) collective-permute-start(bf16[256,512]{1,0:T(8,128)(2,1)S(1)} %get-tuple-element.23.part0.own), channel_id=1, source_target_pairs={{0,4},{4,0},{8,12},{12,8},{16,20},{20,16},{24,28},{28,24},{32,36},... | collective-permute-start | bytes 786440 | tf_op jit(solution)/shard_map/ppermute | solution.py:15
  23.6 14.6 %collective-permute-start = (bf16[256,512]{1,0:T(8,128)(2,1)S(1)}, bf16[256,512]{1,0:T(8,128)(2,1)S(1)}, u32[]{:S(2)}, u32[]{:S(2)}) collective-permute-start(bf16[256,512]{1,0:T(8,128)(2,1)S(1)} %get-tuple-element.23.part0.own), channel_id=1, source_target_pairs={{0,1},{1,0},{2,3},{3,2},{4,5},{5,4},{6,7},{7,6},{8,9},{9,8},{10,11... | collective-permute-start | bytes 786440 | tf_op jit(solution)/shard_map/ppermute | solution.py:15
  27.6 12.3 %collective-permute-start.2 = (bf16[256,512]{1,0:T(8,128)(2,1)S(1)}, bf16[256,512]{1,0:T(8,128)(2,1)S(1)}, u32[]{:S(2)}, u32[]{:S(2)}) collective-permute-start(bf16[256,512]{1,0:T(8,128)(2,1)S(1)} %collective-permute-done.1.part2), channel_id=1, source_target_pairs={{0,1},{1,0},{2,3},{3,2},{4,5},{5,4},{6,7},{7,6},{8,9},{9,8},{10,11... | collective-permute-start | bytes 786440 | tf_op jit(solution)/shard_map/ppermute | solution.py:15
  29.5 1.1 %copy-start = (bf16[3,2,4,128,128]{4,3,2,1,0:T(8,128)(2,1)S(1)}, bf16[3,2,4,128,128]{4,3,2,1,0:T(8,128)(2,1)}, u32[]{:S(2)}) copy-start(bf16[3,2,4,128,128]{4,3,2,1,0:T(8,128)(2,1)} %off_tiles.3) | copy-start | bytes 2359300
  30.7 24.4 %copy-start.2 = (f32[256,512]{1,0:T(8,128)S(1)}, f32[256,512]{1,0:T(8,128)}, u32[]{:S(2)}) copy-start(f32[256,512]{1,0:T(8,128)} %vectors.3) | copy-start | bytes 1572868
  30.7 24.4 %copy-start.3 = (f32[256,512]{1,0:T(8,128)S(1)}, f32[256,512]{1,0:T(8,128)}, u32[]{:S(2)}) copy-start(f32[256,512]{1,0:T(8,128)} %previous.1) | copy-start | bytes 1572868
  32.8 20.2 %collective-permute-start.9 = (bf16[256,512]{1,0:T(8,128)(2,1)S(1)}, bf16[256,512]{1,0:T(8,128)(2,1)S(1)}, u32[]{:S(2)}, u32[]{:S(2)}) collective-permute-start(bf16[256,512]{1,0:T(8,128)(2,1)S(1)} %get-tuple-element.29), channel_id=1, source_target_pairs={{0,1},{1,0},{2,3},{3,2},{4,5},{5,4},{6,7},{7,6},{8,9},{9,8},{10,11... | collective-permute-start | bytes 786440 | tf_op jit(solution)/shard_map/ppermute | solution.py:15
  36.2 18.9 %collective-permute-start.6 = (bf16[256,512]{1,0:T(8,128)(2,1)S(1)}, bf16[256,512]{1,0:T(8,128)(2,1)S(1)}, u32[]{:S(2)}, u32[]{:S(2)}) collective-permute-start(bf16[256,512]{1,0:T(8,128)(2,1)S(1)} %get-tuple-element.26), channel_id=1, source_target_pairs={{0,1},{1,0},{2,3},{3,2},{4,5},{5,4},{6,7},{7,6},{8,9},{9,8},{10,11... | collective-permute-start | bytes 786440 | tf_op jit(solution)/shard_map/ppermute | solution.py:15
  41.1 15.0 %collective-permute-start.7 = (bf16[256,512]{1,0:T(8,128)(2,1)S(1)}, bf16[256,512]{1,0:T(8,128)(2,1)S(1)}, u32[]{:S(2)}, u32[]{:S(2)}) collective-permute-start(bf16[256,512]{1,0:T(8,128)(2,1)S(1)} %get-tuple-element.27), channel_id=1, source_target_pairs={{0,4},{4,0},{8,12},{12,8},{16,20},{20,16},{24,28},{28,24},{32,36},... | collective-permute-start | bytes 786440 | tf_op jit(solution)/shard_map/ppermute | solution.py:15
  43.8 12.3 %collective-permute-start.8 = (bf16[256,512]{1,0:T(8,128)(2,1)S(1)}, bf16[256,512]{1,0:T(8,128)(2,1)S(1)}, u32[]{:S(2)}, u32[]{:S(2)}) collective-permute-start(bf16[256,512]{1,0:T(8,128)(2,1)S(1)} %get-tuple-element.28), channel_id=1, source_target_pairs={{0,32},{4,36},{8,40},{12,44},{16,48},{20,52},{24,56},{28,60},{32,0... | collective-permute-start | bytes 786440 | tf_op jit(solution)/shard_map/ppermute | solution.py:15
  46.0 15.3 %collective-permute-start.11 = (bf16[256,512]{1,0:T(8,128)(2,1)S(1)}, bf16[256,512]{1,0:T(8,128)(2,1)S(1)}, u32[]{:S(2)}, u32[]{:S(2)}) collective-permute-start(bf16[256,512]{1,0:T(8,128)(2,1)S(1)} %get-tuple-element.30), channel_id=1, source_target_pairs={{0,256},{4,260},{8,264},{12,268},{16,272},{20,276},{24,280},{28,28... | collective-permute-start | bytes 786440 | tf_op jit(solution)/shard_map/ppermute | solution.py:15
  53.2 15.7 %collective-permute-start.10 = (bf16[256,512]{1,0:T(8,128)(2,1)S(1)}, bf16[256,512]{1,0:T(8,128)(2,1)S(1)}, u32[]{:S(2)}, u32[]{:S(2)}) collective-permute-start(bf16[256,512]{1,0:T(8,128)(2,1)S(1)} %add_convert_fusion), channel_id=1, source_target_pairs={{0,2},{1,3},{2,0},{3,1},{4,6},{5,7},{6,4},{7,5},{8,10},{9,11},{10,... | collective-permute-start | bytes 786440 | tf_op jit(solution)/shard_map/ppermute | solution.py:15

commit v3 on v2

--- a/solution.py
+++ b/solution.py
@@ -113,10 +113,12 @@
     for strip in range(strips):
         rows = pl.ds(strip * size, size)
         total = acc[rows, :] + got1[rows, :].astype(jnp.float32)
+        tiles, blocks = [], []
         for slot in range(slots):
             place = pl.multiple_of((diag_cols[strip, slot] ^ shift) * size, size)
-            tile = live(diag_tiles[strip, slot], diag_mask[strip, slot])
-            total = total + dot_plain(tile, gathered[pl.ds(place, size), :])
+            tiles.append(live(diag_tiles[strip, slot], diag_mask[strip, slot]))
+            blocks.append(gathered[pl.ds(place, size), :])
+        total = total + dot_plain(jnp.concatenate(tiles, 1), jnp.concatenate(blocks, 0))
         base[rows, :] = 2.0 / cheb_half * (total - cheb_center * vectors[rows, :]) - previous[rows, :]
 
 

time: 70.3 us -> 70.3 us (level)
  no operation moved by 1% of the time
where the time goes in v3:
time: 70.3 us; the launch traced here: 69.8 us
  starting transfers between devices  47.2 us (67%)
  waiting for transfers between devices  14.5 us (21%)
  Pallas kernels  5.7 us (8%)
  local copies, waits for them, and re-layouts  1.14 us (2%)
  other arithmetic  1.04 us (1%)
    ppermute x12, starting transfers between devices, swap(): return lax.ppermute(block, axis, [(i, i ^ mask) for i in range(count)])  47.2 us
    ppermute x12, waiting for transfers between devices, swap(): return lax.ppermute(block, axis, [(i, i ^ mask) for i in range(count)])  14.5 us
    pallas_call x4, Pallas kernels, call(): pl.pallas_call(kernel, in_specs=[smem] * len(scalars) + [vmem] * len(arra...  5.7 us
  transfers between devices with their start and end apart: 12, of which 3 were waited for; matrix products, arithmetic and copies ran while one was open for 0% of the time, Pallas kernels for 6%

profile of v3, /device:TPU:1, one launch (start us, length us, event | category | flops | bytes accessed | tf_op | source)
XLA Modules:
  0.0 69.8 jit_solution(1742111632801762736)
XLA Ops:
  0.0 1.4 %shard_map.82 = (bf16[256,512]{1,0:T(8,128)(2,1)S(1)}, bf16[2,4,128,128]{3,2,1,0:T(8,128)(2,1)S(1)}, s32[2,4]{1,0:T(2,128)S(1)}, s32[2,4]{1,0:T(2,128)S(1)}, s32...) custom-call(f32[256,512]{1,0:T(8,128)} %vectors.3, bf16[2,4,128,128]{3,2,1,0:T(8,128)(2,1)} %refs_0_.1, s32[2,4]{1,0:T(2,128)} %refs_1_.1, ...), custom_call_target="tpu_custom_call" | custom-call | tf_op jit(solution)/shard_map/pallas_call | solution.py:139
  1.4 6.6 %collective-permute-start.1 = (bf16[256,512]{1,0:T(8,128)(2,1)S(1)}, bf16[256,512]{1,0:T(8,128)(2,1)S(1)}, u32[]{:S(2)}, u32[]{:S(2)}) collective-permute-start(bf16[256,512]{1,0:T(8,128)(2,1)S(1)} %get-tuple-element.23.part0.own), channel_id=1, source_target_pairs={{0,2},{1,3},{2,0},{3,1},{4,6},{5,7},{6,4},{7,5},{8,10},{9,11},{10,... | collective-permute-start | bytes 786440 | tf_op jit(solution)/shard_map/ppermute | solution.py:15
  8.0 7.5 %collective-permute-start.5 = (bf16[256,512]{1,0:T(8,128)(2,1)S(1)}, bf16[256,512]{1,0:T(8,128)(2,1)S(1)}, u32[]{:S(2)}, u32[]{:S(2)}) collective-permute-start(bf16[256,512]{1,0:T(8,128)(2,1)S(1)} %get-tuple-element.23.part0.own), channel_id=1, source_target_pairs={{0,256},{4,260},{8,264},{12,268},{16,272},{20,276},{24,280},{28,28... | collective-permute-start | bytes 786440 | tf_op jit(solution)/shard_map/ppermute | solution.py:15
  15.5 4.7 %collective-permute-start.4 = (bf16[256,512]{1,0:T(8,128)(2,1)S(1)}, bf16[256,512]{1,0:T(8,128)(2,1)S(1)}, u32[]{:S(2)}, u32[]{:S(2)}) collective-permute-start(bf16[256,512]{1,0:T(8,128)(2,1)S(1)} %get-tuple-element.23.part0.own), channel_id=1, source_target_pairs={{0,32},{4,36},{8,40},{12,44},{16,48},{20,52},{24,56},{28,60},{32,0... | collective-permute-start | bytes 786440 | tf_op jit(solution)/shard_map/ppermute | solution.py:15
  20.1 3.4 %collective-permute-start.3 = (bf16[256,512]{1,0:T(8,128)(2,1)S(1)}, bf16[256,512]{1,0:T(8,128)(2,1)S(1)}, u32[]{:S(2)}, u32[]{:S(2)}) collective-permute-start(bf16[256,512]{1,0:T(8,128)(2,1)S(1)} %get-tuple-element.23.part0.own), channel_id=1, source_target_pairs={{0,4},{4,0},{8,12},{12,8},{16,20},{20,16},{24,28},{28,24},{32,36},... | collective-permute-start | bytes 786440 | tf_op jit(solution)/shard_map/ppermute | solution.py:15
  23.6 4.0 %collective-permute-start = (bf16[256,512]{1,0:T(8,128)(2,1)S(1)}, bf16[256,512]{1,0:T(8,128)(2,1)S(1)}, u32[]{:S(2)}, u32[]{:S(2)}) collective-permute-start(bf16[256,512]{1,0:T(8,128)(2,1)S(1)} %get-tuple-element.23.part0.own), channel_id=1, source_target_pairs={{0,1},{1,0},{2,3},{3,2},{4,5},{5,4},{6,7},{7,6},{8,9},{9,8},{10,11... | collective-permute-start | bytes 786440 | tf_op jit(solution)/shard_map/ppermute | solution.py:15
  27.6 0.0 collective-permute-done.1.part2
  27.6 1.9 %collective-permute-start.2 = (bf16[256,512]{1,0:T(8,128)(2,1)S(1)}, bf16[256,512]{1,0:T(8,128)(2,1)S(1)}, u32[]{:S(2)}, u32[]{:S(2)}) collective-permute-start(bf16[256,512]{1,0:T(8,128)(2,1)S(1)} %collective-permute-done.1.part2), channel_id=1, source_target_pairs={{0,1},{1,0},{2,3},{3,2},{4,5},{5,4},{6,7},{7,6},{8,9},{9,8},{10,11... | collective-permute-start | bytes 786440 | tf_op jit(solution)/shard_map/ppermute | solution.py:15
  29.5 0.0 collective-permute-done.5.arr2
  29.5 0.0 collective-permute-done.4.arr1
  29.5 0.0 collective-permute-done.3.arr0
  29.5 0.0 copy-start
  29.5 1.1 %copy-done = bf16[3,2,4,128,128]{4,3,2,1,0:T(8,128)(2,1)S(1)} copy-done((bf16[3,2,4,128,128]{4,3,2,1,0:T(8,128)(2,1)S(1)}, bf16[3,2,4,128,128]{4,3,2,1,0:T(8,128)(2,1)}, u32[]{:S(2)}) %copy-start) | copy-done | bytes 786456
  30.7 2.2 %shard_map.84 = (f32[1024,512]{1,0:T(8,128)S(1)}, bf16[256,512]{1,0:T(8,128)(2,1)S(1)}, bf16[256,512]{1,0:T(8,128)(2,1)S(1)}) custom-call(s32[2,4]{1,0:T(2,128)S(1)} %get-tuple-element.18.diag_cols, s32[2,4]{1,0:T(2,128)S(1)} %get-tuple-element.19.diag_mask, s32[3,2,4]{2,1,0:T(2,128)S(1)} %get-tuple-element.21.off_rows, ...), custom_call_target="tpu_custom_call" | custom-call | tf_op jit(solution)/shard_map/pallas_call | solution.py:139
  32.8 3.4 %collective-permute-start.9 = (bf16[256,512]{1,0:T(8,128)(2,1)S(1)}, bf16[256,512]{1,0:T(8,128)(2,1)S(1)}, u32[]{:S(2)}, u32[]{:S(2)}) collective-permute-start(bf16[256,512]{1,0:T(8,128)(2,1)S(1)} %get-tuple-element.29), channel_id=1, source_target_pairs={{0,1},{1,0},{2,3},{3,2},{4,5},{5,4},{6,7},{7,6},{8,9},{9,8},{10,11... | collective-permute-start | bytes 786440 | tf_op jit(solution)/shard_map/ppermute | solution.py:15
  36.2 1.9 %collective-permute-start.6 = (bf16[256,512]{1,0:T(8,128)(2,1)S(1)}, bf16[256,512]{1,0:T(8,128)(2,1)S(1)}, u32[]{:S(2)}, u32[]{:S(2)}) collective-permute-start(bf16[256,512]{1,0:T(8,128)(2,1)S(1)} %get-tuple-element.26), channel_id=1, source_target_pairs={{0,1},{1,0},{2,3},{3,2},{4,5},{5,4},{6,7},{7,6},{8,9},{9,8},{10,11... | collective-permute-start | bytes 786440 | tf_op jit(solution)/shard_map/ppermute | solution.py:15
  38.1 0.0 collective-permute-done.part1
  38.1 1.7 %collective-permute-done.2.part3 = bf16[256,512]{1,0:T(8,128)(2,1)S(1)} collective-permute-done((bf16[256,512]{1,0:T(8,128)(2,1)S(1)}, bf16[256,512]{1,0:T(8,128)(2,1)S(1)}, u32[]{:S(2)}, u32[]{:S(2)}) %collective-permute-start.2) | collective-permute-done | bytes 262176 | tf_op jit(solution)/shard_map/ppermute | solution.py:15
  39.8 1.3 %shard_map.83 = (bf16[1024,512]{1,0:T(8,128)(2,1)S(1)}, bf16[256,512]{1,0:T(8,128)(2,1)S(1)}, bf16[256,512]{1,0:T(8,128)(2,1)S(1)}, bf16[256,512]{1,0:T(8,128)(2,1)S(1)}) custom-call(s32[3,2,4]{2,1,0:T(2,128)S(1)} %get-tuple-element.21.off_rows, s32[3,2,4]{2,1,0:T(2,128)S(1)} %get-tuple-element.22.off_mask, bf16[3,2,4,128,128]{4,3,2,1,0:T(8,128)(2,1)S(1)} %copy-done.1, ...), custom_call_target="tpu_custom_call" | custom-call | tf_op jit(solution)/shard_map/pallas_call | solution.py:139
  41.1 2.7 %collective-permute-start.7 = (bf16[256,512]{1,0:T(8,128)(2,1)S(1)}, bf16[256,512]{1,0:T(8,128)(2,1)S(1)}, u32[]{:S(2)}, u32[]{:S(2)}) collective-permute-start(bf16[256,512]{1,0:T(8,128)(2,1)S(1)} %get-tuple-element.27), channel_id=1, source_target_pairs={{0,4},{4,0},{8,12},{12,8},{16,20},{20,16},{24,28},{28,24},{32,36},... | collective-permute-start | bytes 786440 | tf_op jit(solution)/shard_map/ppermute | solution.py:15
  43.8 2.1 %collective-permute-start.8 = (bf16[256,512]{1,0:T(8,128)(2,1)S(1)}, bf16[256,512]{1,0:T(8,128)(2,1)S(1)}, u32[]{:S(2)}, u32[]{:S(2)}) collective-permute-start(bf16[256,512]{1,0:T(8,128)(2,1)S(1)} %get-tuple-element.28), channel_id=1, source_target_pairs={{0,32},{4,36},{8,40},{12,44},{16,48},{20,52},{24,56},{28,60},{32,0... | collective-permute-start | bytes 786440 | tf_op jit(solution)/shard_map/ppermute | solution.py:15
  46.0 7.1 %collective-permute-start.11 = (bf16[256,512]{1,0:T(8,128)(2,1)S(1)}, bf16[256,512]{1,0:T(8,128)(2,1)S(1)}, u32[]{:S(2)}, u32[]{:S(2)}) collective-permute-start(bf16[256,512]{1,0:T(8,128)(2,1)S(1)} %get-tuple-element.30), channel_id=1, source_target_pairs={{0,256},{4,260},{8,264},{12,268},{16,272},{20,276},{24,280},{28,28... | collective-permute-start | bytes 786440 | tf_op jit(solution)/shard_map/ppermute | solution.py:15
  53.1 0.0 collective-permute-done.9
  53.1 0.1 add_convert_fusion
  53.2 1.9 %collective-permute-start.10 = (bf16[256,512]{1,0:T(8,128)(2,1)S(1)}, bf16[256,512]{1,0:T(8,128)(2,1)S(1)}, u32[]{:S(2)}, u32[]{:S(2)}) collective-permute-start(bf16[256,512]{1,0:T(8,128)(2,1)S(1)} %add_convert_fusion), channel_id=1, source_target_pairs={{0,2},{1,3},{2,0},{3,1},{4,6},{5,7},{6,4},{7,5},{8,10},{9,11},{10,... | collective-permute-start | bytes 786440 | tf_op jit(solution)/shard_map/ppermute | solution.py:15
  55.1 0.0 collective-permute-done.6.got1
  55.1 0.9 %shard_map.85 = f32[256,512]{1,0:T(8,128)S(1)} custom-call(s32[2,4]{1,0:T(2,128)S(1)} %get-tuple-element.18.diag_cols, s32[2,4]{1,0:T(2,128)S(1)} %get-tuple-element.19.diag_mask, bf16[2,4,128,128]{3,2,1,0:T(8,128)(2,1)S(1)} %get-tuple-element.20.diag_tiles, bf16[1024,512]{1,0:T(8,128)(2,1)S(1)} %get-tuple-element.24.gathered, ...), custom_call_target="tpu_custom_call" | custom-call | tf_op jit(solution)/shard_map/pallas_call | solution.py:139
  56.0 0.0 collective-permute-done.7
  56.0 0.0 collective-permute-done.8
  56.1 5.2 %collective-permute-done.11 = bf16[256,512]{1,0:T(8,128)(2,1)S(1)} collective-permute-done((bf16[256,512]{1,0:T(8,128)(2,1)S(1)}, bf16[256,512]{1,0:T(8,128)(2,1)S(1)}, u32[]{:S(2)}, u32[]{:S(2)}) %collective-permute-start.11) | collective-permute-done | bytes 262176 | tf_op jit(solution)/shard_map/ppermute | solution.py:15
  61.2 7.6 %collective-permute-done.10 = bf16[256,512]{1,0:T(8,128)(2,1)S(1)} collective-permute-done((bf16[256,512]{1,0:T(8,128)(2,1)S(1)}, bf16[256,512]{1,0:T(8,128)(2,1)S(1)}, u32[]{:S(2)}, u32[]{:S(2)}) %collective-permute-start.10) | collective-permute-done | bytes 262176 | tf_op jit(solution)/shard_map/ppermute | solution.py:15
  68.9 1.0 %convert_add_fusion = f32[256,512]{1,0:T(8,128)} fusion(bf16[256,512]{1,0:T(8,128)(2,1)S(1)} %collective-permute-done.11, bf16[256,512]{1,0:T(8,128)(2,1)S(1)} %collective-permute-done.10, bf16[256,512]{1,0:T(8,128)(2,1)S(1)} %collective-permute-done.8, f32[256,512]{1,0:T(8,128)S(1)} %shard_map.85, bf16[256,512]{1,0:T(8,128)(2,1)S(1)} %collective-permute-done.7), kind=kLoop, calls=%fused_computation | loop fusion | flops 1048576 | bytes 2097152 | tf_op jit(solution)/shard_map/add | solution.py:197
  (6 shorter events, 0.0 us)
Async XLA Ops:
  0.0 39.8 %copy-start.1 = (bf16[3,2,4,128,128]{4,3,2,1,0:T(8,128)(2,1)S(1)}, bf16[3,2,4,128,128]{4,3,2,1,0:T(8,128)(2,1)}, u32[]{:S(2)}) copy-start(bf16[3,2,4,128,128]{4,3,2,1,0:T(8,128)(2,1)} %off_tiles.3) | copy-start | bytes 2359300
  1.4 26.2 %collective-permute-start.1 = (bf16[256,512]{1,0:T(8,128)(2,1)S(1)}, bf16[256,512]{1,0:T(8,128)(2,1)S(1)}, u32[]{:S(2)}, u32[]{:S(2)}) collective-permute-start(bf16[256,512]{1,0:T(8,128)(2,1)S(1)} %get-tuple-element.23.part0.own), channel_id=1, source_target_pairs={{0,2},{1,3},{2,0},{3,1},{4,6},{5,7},{6,4},{7,5},{8,10},{9,11},{10,... | collective-permute-start | bytes 786440 | tf_op jit(solution)/shard_map/ppermute | solution.py:15
  8.0 21.5 %collective-permute-start.5 = (bf16[256,512]{1,0:T(8,128)(2,1)S(1)}, bf16[256,512]{1,0:T(8,128)(2,1)S(1)}, u32[]{:S(2)}, u32[]{:S(2)}) collective-permute-start(bf16[256,512]{1,0:T(8,128)(2,1)S(1)} %get-tuple-element.23.part0.own), channel_id=1, source_target_pairs={{0,256},{4,260},{8,264},{12,268},{16,272},{20,276},{24,280},{28,28... | collective-permute-start | bytes 786440 | tf_op jit(solution)/shard_map/ppermute | solution.py:15
  15.5 14.1 %collective-permute-start.4 = (bf16[256,512]{1,0:T(8,128)(2,1)S(1)}, bf16[256,512]{1,0:T(8,128)(2,1)S(1)}, u32[]{:S(2)}, u32[]{:S(2)}) collective-permute-start(bf16[256,512]{1,0:T(8,128)(2,1)S(1)} %get-tuple-element.23.part0.own), channel_id=1, source_target_pairs={{0,32},{4,36},{8,40},{12,44},{16,48},{20,52},{24,56},{28,60},{32,0... | collective-permute-start | bytes 786440 | tf_op jit(solution)/shard_map/ppermute | solution.py:15
  20.1 9.4 %collective-permute-start.3 = (bf16[256,512]{1,0:T(8,128)(2,1)S(1)}, bf16[256,512]{1,0:T(8,128)(2,1)S(1)}, u32[]{:S(2)}, u32[]{:S(2)}) collective-permute-start(bf16[256,512]{1,0:T(8,128)(2,1)S(1)} %get-tuple-element.23.part0.own), channel_id=1, source_target_pairs={{0,4},{4,0},{8,12},{12,8},{16,20},{20,16},{24,28},{28,24},{32,36},... | collective-permute-start | bytes 786440 | tf_op jit(solution)/shard_map/ppermute | solution.py:15
  23.6 14.6 %collective-permute-start = (bf16[256,512]{1,0:T(8,128)(2,1)S(1)}, bf16[256,512]{1,0:T(8,128)(2,1)S(1)}, u32[]{:S(2)}, u32[]{:S(2)}) collective-permute-start(bf16[256,512]{1,0:T(8,128)(2,1)S(1)} %get-tuple-element.23.part0.own), channel_id=1, source_target_pairs={{0,1},{1,0},{2,3},{3,2},{4,5},{5,4},{6,7},{7,6},{8,9},{9,8},{10,11... | collective-permute-start | bytes 786440 | tf_op jit(solution)/shard_map/ppermute | solution.py:15
  27.6 12.3 %collective-permute-start.2 = (bf16[256,512]{1,0:T(8,128)(2,1)S(1)}, bf16[256,512]{1,0:T(8,128)(2,1)S(1)}, u32[]{:S(2)}, u32[]{:S(2)}) collective-permute-start(bf16[256,512]{1,0:T(8,128)(2,1)S(1)} %collective-permute-done.1.part2), channel_id=1, source_target_pairs={{0,1},{1,0},{2,3},{3,2},{4,5},{5,4},{6,7},{7,6},{8,9},{9,8},{10,11... | collective-permute-start | bytes 786440 | tf_op jit(solution)/shard_map/ppermute | solution.py:15
  29.5 1.1 %copy-start = (bf16[3,2,4,128,128]{4,3,2,1,0:T(8,128)(2,1)S(1)}, bf16[3,2,4,128,128]{4,3,2,1,0:T(8,128)(2,1)}, u32[]{:S(2)}) copy-start(bf16[3,2,4,128,128]{4,3,2,1,0:T(8,128)(2,1)} %off_tiles.3) | copy-start | bytes 2359300
  30.7 24.4 %copy-start.2 = (f32[256,512]{1,0:T(8,128)S(1)}, f32[256,512]{1,0:T(8,128)}, u32[]{:S(2)}) copy-start(f32[256,512]{1,0:T(8,128)} %vectors.3) | copy-start | bytes 1572868
  30.7 24.4 %copy-start.3 = (f32[256,512]{1,0:T(8,128)S(1)}, f32[256,512]{1,0:T(8,128)}, u32[]{:S(2)}) copy-start(f32[256,512]{1,0:T(8,128)} %previous.1) | copy-start | bytes 1572868
  32.8 20.2 %collective-permute-start.9 = (bf16[256,512]{1,0:T(8,128)(2,1)S(1)}, bf16[256,512]{1,0:T(8,128)(2,1)S(1)}, u32[]{:S(2)}, u32[]{:S(2)}) collective-permute-start(bf16[256,512]{1,0:T(8,128)(2,1)S(1)} %get-tuple-element.29), channel_id=1, source_target_pairs={{0,1},{1,0},{2,3},{3,2},{4,5},{5,4},{6,7},{7,6},{8,9},{9,8},{10,11... | collective-permute-start | bytes 786440 | tf_op jit(solution)/shard_map/ppermute | solution.py:15
  36.2 18.9 %collective-permute-start.6 = (bf16[256,512]{1,0:T(8,128)(2,1)S(1)}, bf16[256,512]{1,0:T(8,128)(2,1)S(1)}, u32[]{:S(2)}, u32[]{:S(2)}) collective-permute-start(bf16[256,512]{1,0:T(8,128)(2,1)S(1)} %get-tuple-element.26), channel_id=1, source_target_pairs={{0,1},{1,0},{2,3},{3,2},{4,5},{5,4},{6,7},{7,6},{8,9},{9,8},{10,11... | collective-permute-start | bytes 786440 | tf_op jit(solution)/shard_map/ppermute | solution.py:15
  41.1 14.9 %collective-permute-start.7 = (bf16[256,512]{1,0:T(8,128)(2,1)S(1)}, bf16[256,512]{1,0:T(8,128)(2,1)S(1)}, u32[]{:S(2)}, u32[]{:S(2)}) collective-permute-start(bf16[256,512]{1,0:T(8,128)(2,1)S(1)} %get-tuple-element.27), channel_id=1, source_target_pairs={{0,4},{4,0},{8,12},{12,8},{16,20},{20,16},{24,28},{28,24},{32,36},... | collective-permute-start | bytes 786440 | tf_op jit(solution)/shard_map/ppermute | solution.py:15
  43.8 12.2 %collective-permute-start.8 = (bf16[256,512]{1,0:T(8,128)(2,1)S(1)}, bf16[256,512]{1,0:T(8,128)(2,1)S(1)}, u32[]{:S(2)}, u32[]{:S(2)}) collective-permute-start(bf16[256,512]{1,0:T(8,128)(2,1)S(1)} %get-tuple-element.28), channel_id=1, source_target_pairs={{0,32},{4,36},{8,40},{12,44},{16,48},{20,52},{24,56},{28,60},{32,0... | collective-permute-start | bytes 786440 | tf_op jit(solution)/shard_map/ppermute | solution.py:15
  46.0 15.3 %collective-permute-start.11 = (bf16[256,512]{1,0:T(8,128)(2,1)S(1)}, bf16[256,512]{1,0:T(8,128)(2,1)S(1)}, u32[]{:S(2)}, u32[]{:S(2)}) collective-permute-start(bf16[256,512]{1,0:T(8,128)(2,1)S(1)} %get-tuple-element.30), channel_id=1, source_target_pairs={{0,256},{4,260},{8,264},{12,268},{16,272},{20,276},{24,280},{28,28... | collective-permute-start | bytes 786440 | tf_op jit(solution)/shard_map/ppermute | solution.py:15
  53.2 15.7 %collective-permute-start.10 = (bf16[256,512]{1,0:T(8,128)(2,1)S(1)}, bf16[256,512]{1,0:T(8,128)(2,1)S(1)}, u32[]{:S(2)}, u32[]{:S(2)}) collective-permute-start(bf16[256,512]{1,0:T(8,128)(2,1)S(1)} %add_convert_fusion), channel_id=1, source_target_pairs={{0,2},{1,3},{2,0},{3,1},{4,6},{5,7},{6,4},{7,5},{8,10},{9,11},{10,... | collective-permute-start | bytes 786440 | tf_op jit(solution)/shard_map/ppermute | solution.py:15
